TPU v7x, 512 devices: a whole 4x8x8 slice. The times are simulated.
512 devices in a mesh: seq: 64 (over z, x, core), exp: 8 (over y).
Axes of the slice: x: 4, y: 8, z: 8, core: 2. Of those that a mesh axis runs over, the one named last changes fastest.
Arguments:
- inner_x: bfloat16 [8192, 8192], P('seq', 'exp'), may hold values from -6 to 6
- inner_z: bfloat16 [8192, 8192], P('seq', 'exp'), may hold values from -6 to 6
- step_raw: bfloat16 [8192, 8192], P('seq', 'exp'), may hold values from -4.5 to 3
- conv_weight: float32 [4, 8192], P(None, 'exp'), may hold values from -3 to 3
- state_proj: bfloat16 [8192, 32], P('exp'), may hold values from -0.125 to 0.125
- step_bias: float32 [8192], P('exp'), may hold values from -7 to -2.3
- decay_log: float32 [16, 8192], P(None, 'exp'), may hold values from -4 to 2.8
- skip_gain: float32 [8192], P('exp'), may hold values from 0.5 to 1.5
- moe_tokens: bfloat16 [8192, 4096], P('seq', 'exp'), may hold values from -6 to 6
- routes: int32 [8192, 2], P('seq'), may hold values from 0 to 15, all different within a row; in each aligned block of 128 rows (0 to 127, 128 to 255, ...) at most 20 rows name the same one
- gate_weight: bfloat16 [8, 12288, 4096], P('exp', 'seq'), may hold values from -0.09375 to 0.09375
- up_weight: bfloat16 [8, 12288, 4096], P('exp', 'seq'), may hold values from -0.09375 to 0.09375
Outputs:
- mixed: bfloat16 [8192, 8192], P('seq', 'exp')
- hidden: bfloat16 [8, 12288, 1280], P('exp', 'seq')
Inputs may be any that keep to these rules, and one draw needn't show every extreme that they name: `routes`: in each aligned block of 128 rows (the tokens of one device), no expert is named by more than 20 rows, a bound that some block reaches; the two choices of a token differ.
All inputs are finite; a program needn't handle non-finite values.
Results may differ from a plain program's by a relative error of at most 0.0051.
Values may be sent and summed in bfloat16 or wider, within the bound.
No kernel may reach another device: no remote copies, remote signals or barrier semaphores. Data moves between devices by JAX's collectives and lax.ppermute only.
A program may use at most 128 MiB of HBM per device.

v0:
```python
import functools

import jax
import jax.numpy as jnp
from jax import lax
from jax.experimental import pallas as pl
from jax.experimental.pallas import tpu as pltpu
from jax.sharding import Mesh
from jax.sharding import PartitionSpec as P

CAP = 20
F32 = jnp.float32
BF16 = jnp.bfloat16
LOG2E = 1.4426950408889634
SEQ = ("z", "x", "c")

VMEM = pl.BlockSpec(memory_space=pltpu.VMEM)
SMEM = pl.BlockSpec(memory_space=pltpu.SMEM)
WHOLE = pl.BlockSpec(memory_space=pltpu.HBM)


def call(kernel, out_shape, in_specs, scratch=(), name=None, vmem=60, flops=0):
    single = not isinstance(out_shape, tuple)
    outs = (out_shape,) if single else out_shape

    def run(*operands):
        moved = [index for index in range(len(in_specs)) if in_specs[index] is WHOLE]
        buffers = [pltpu.VMEM(operands[index].shape, operands[index].dtype) for index in moved]
        buffers += [pltpu.VMEM(out.shape, out.dtype) for out in outs]
        count = len(operands)

        def body(*refs):
            inputs, results = list(refs[:count]), refs[count : count + len(outs)]
            held = refs[count + len(outs) : count + len(outs) + len(buffers)]
            rest, sems = refs[count + len(outs) + len(buffers) : -1], refs[-1]
            copies = []
            for place, index in enumerate(moved):
                copies.append(pltpu.make_async_copy(inputs[index], held[place], sems.at[place]))
                inputs[index] = held[place]
            for copy in copies:
                copy.start()
            for copy in copies:
                copy.wait()
            made = held[len(moved) :]
            kernel(*inputs, *made, *rest)
            copies = [
                pltpu.make_async_copy(source, target, sems.at[len(moved) + place])
                for place, (source, target) in enumerate(zip(made, results))
            ]
            for copy in copies:
                copy.start()
            for copy in copies:
                copy.wait()

        found = pl.pallas_call(
            body,
            out_shape=outs,
            in_specs=in_specs,
            out_specs=(WHOLE,) * len(outs),
            scratch_shapes=[*buffers, *scratch, pltpu.SemaphoreType.DMA((len(buffers),))],
            name=name,
            compiler_params=pltpu.CompilerParams(vmem_limit_bytes=vmem << 20),
            cost_estimate=pl.CostEstimate(flops=flops, transcendentals=0, bytes_accessed=4 << 20),
        )(*operands)
        return found[0] if single else found

    return run


def shape(dims, dtype):
    return jax.ShapeDtypeStruct(dims, dtype)


def place_kernel(routes_ref, tokens_ref, out_ref, wide):
    tokens = tokens_ref.shape[0]
    row = lax.broadcasted_iota(jnp.int32, (256, tokens), 0)
    expert, slot = row >> 5, row & 31
    named = (routes_ref[0:1, :] == expert) | (routes_ref[1:2, :] == expert)
    earlier = lax.broadcasted_iota(jnp.int32, (tokens, tokens), 0) < lax.broadcasted_iota(
        jnp.int32, (tokens, tokens), 1
    )
    before = jnp.dot(
        jnp.where(named, 1.0, 0.0).astype(BF16),
        jnp.where(earlier, 1.0, 0.0).astype(BF16),
        preferred_element_type=F32,
    )
    table = jnp.where(named & (before == slot.astype(F32)), 1.0, 0.0).astype(BF16)
    placed = jnp.dot(table, tokens_ref[...], preferred_element_type=F32)
    for index in range(8):
        rows = placed[index * 32 : index * 32 + CAP]
        wide[:CAP, :], wide[CAP:, :] = rows[:, :256], rows[:, 256:]
        packed = wide[...].astype(BF16)
        for copy in range(4):
            out_ref[index * 4 + copy] = packed


def assemble_kernel(got_ref, out_ref, wide):
    for index in range(32):
        rows = got_ref[index].astype(F32)
        here = pl.ds(index % 4 * CAP, CAP)
        start = index // 4 * 512
        wide[here, start : start + 256] = rows[:CAP]
        wide[here, start + 256 : start + 512] = rows[CAP:]
    out_ref[...] = wide[...].astype(BF16)


def expand_kernel(blocks, pairs, *refs):
    inputs = blocks + 2 * pairs
    sources, outs, refs = refs[:inputs], refs[inputs : inputs + pairs], refs[inputs + pairs :]
    rows, held, made, sems = refs[0], refs[1 : 1 + pairs], refs[1 + pairs : -1], refs[-1]
    copies, start = [], 0
    for source in sources[:blocks]:
        size = source.shape[0]
        copies.append((source, rows.at[pl.ds(start, size)]))
        start += size
    units = made[0].shape[0]
    for index, source in enumerate(sources[blocks:]):
        target = held[index // 2].at[pl.ds(index % 2 * units, units)]
        copies.append((source, target))
    copies = [
        pltpu.make_async_copy(source, target, sems.at[index])
        for index, (source, target) in enumerate(copies)
    ]
    for copy in copies[blocks:] + copies[:blocks]:
        copy.start()
    for copy in copies[:blocks]:
        copy.wait()
    sent = []
    for index, (weight, hidden, out) in enumerate(zip(held, made, outs)):
        for copy in copies[blocks + 2 * index : blocks + 2 * index + 2]:
            copy.wait()
        both = lax.dot_general(
            weight[...], rows[...], (((1,), (1,)), ((), ())), preferred_element_type=F32
        )
        hidden[...] = (silu(both[:units]) * both[units:]).astype(BF16)
        sent.append(pltpu.make_async_copy(hidden, out, sems.at[inputs + index]))
        sent[-1].start()
    for copy in sent:
        copy.wait()


def expand(blocks, pairs, name):
    weights = [weight for pair in pairs for weight in pair]
    units, count = weights[0].shape[0], sum(block.shape[0] for block in blocks)
    out = shape((units, count), BF16)
    total = len(pairs)
    return pl.pallas_call(
        functools.partial(expand_kernel, len(blocks), total),
        out_shape=(out,) * total,
        in_specs=[WHOLE] * (len(blocks) + 2 * total),
        out_specs=(WHOLE,) * total,
        scratch_shapes=[
            pltpu.VMEM((count, 4096), BF16),
            *[pltpu.VMEM((2 * units, 4096), BF16)] * total,
            *[pltpu.VMEM(out.shape, BF16)] * total,
            pltpu.SemaphoreType.DMA((len(blocks) + 3 * total,)),
        ],
        name=name,
        compiler_params=pltpu.CompilerParams(vmem_limit_bytes=60 << 20),
        cost_estimate=pl.CostEstimate(
            flops=4 * total * units * count * 4096, transcendentals=0, bytes_accessed=8 << 20
        ),
    )(*blocks, *weights)


def divided(value, by):
    return (value * (65536 // by + 1)) >> 16


EARLY = ((0, 0), (1, 0), (1, 1), (2, 0), (2, 1))
LATE = ((3, 0), (3, 1), (4, 0))


def order_kernel(place_ref, mine_early, mine_late, other_early, other_late, out_ref):
    columns = out_ref.shape[1]
    total = jnp.zeros(out_ref.shape, F32)
    for pair, blocks in (((mine_early, other_early), EARLY), ((mine_late, other_late), LATE)):
        count = pair[0].shape[1]
        row = lax.broadcasted_iota(jnp.int32, (count, 1), 0)
        block = divided(row, 4 * CAP)
        within = row - block * (4 * CAP)
        steps, twin = (jnp.full_like(row, value) for value in blocks[0])
        for index, (step, other) in enumerate(blocks[1:], 1):
            steps = jnp.where(block == index, step, steps)
            twin = jnp.where(block == index, other, twin)
        base = within + divided(within, CAP) * CAP
        column = lax.broadcasted_iota(jnp.int32, (count, columns), 1)
        for ref, holder in zip(pair, (place_ref[1], 1 - place_ref[1])):
            layer = (place_ref[0] + steps * (2 * holder - 1)) & 7
            core = holder + twin * (1 - 2 * holder)
            target = layer * (8 * CAP) + core * CAP + base
            table = jnp.where(column == target, 1.0, 0.0).astype(BF16)
            total = total + jnp.dot(ref[...], table, preferred_element_type=F32)
    out_ref[...] = total.astype(BF16)


def silu(value):
    return value / (1.0 + jnp.exp(-value))


def softplus(value):
    small = jnp.exp(-jnp.abs(value))
    ratio = small / (2.0 + small)
    square = ratio * ratio
    series = jnp.full_like(square, 1.0 / 15.0)
    for odd in (13, 11, 9, 7, 5, 3):
        series = series * square + 1.0 / odd
    return jnp.maximum(value, 0.0) + 2.0 * ratio * (series * square + 1.0)


def conv_kernel(
    x_ref,
    rim_ref,
    raw_ref,
    weight_ref,
    proj_ref,
    bias_ref,
    decay_ref,
    conv_ref,
    step_ref,
    drive_ref,
    rate_ref,
    part_ref,
    padded,
):
    rows, width = x_ref.shape
    padded[8:, :] = x_ref[...].astype(F32)
    padded[5:8, :] = rim_ref[...].astype(F32)
    total = jnp.zeros((rows, width), F32)
    for tap in range(4):
        total = total + weight_ref[tap : tap + 1, :] * padded[5 + tap : 5 + tap + rows, :]
    conv = silu(total)
    conv_ref[...] = conv
    part = lax.dot_general(
        proj_ref[...], conv.astype(BF16), (((1,), (1,)), ((), ())), preferred_element_type=F32
    )
    for index in range(8):
        part_ref[index] = part
    step = softplus(raw_ref[...].astype(F32) + bias_ref[...])
    drive = step * conv
    rate = -jnp.exp(decay_ref[...]) * LOG2E
    for index in range(width // 128):
        lanes = slice(index * 128, index * 128 + 128)
        step_ref[pl.ds(index, rows, stride=8), :] = step[:, lanes]
        drive_ref[pl.ds(index, rows, stride=8), :] = drive[:, lanes]
        rate_ref[pl.ds(index, rate.shape[0], stride=8), :] = rate[:, lanes]


def pack_state(states, total):
    high = total.astype(BF16).astype(F32)
    middle = (total - high).astype(BF16).astype(F32)
    low = total - high - middle
    tail = jnp.concatenate([high, middle, low, jnp.zeros_like(total)], axis=0)
    return jnp.concatenate(list(states) + [tail], axis=0).astype(BF16)


def unpack_state(ref, position):
    block = ref[position].astype(F32)
    states = [block[n * 8 : n * 8 + 8] for n in range(16)]
    return states, block[128:136] + block[136:144] + block[144:152]


def scan_kernel(coef_ref, step_ref, drive_ref, rate_ref, y_ref, sum_ref, end_ref):
    rows = step_ref.shape[0] // 8
    rates = [rate_ref[n * 8 : n * 8 + 8, :] for n in range(16)]
    zero = jnp.zeros((8, 128), F32)

    def advance(token, carry):
        total, states = carry
        here = pl.ds(pl.multiple_of(token * 8, 8), 8)
        step, drive = step_ref[here, :], drive_ref[here, :]
        total = total + step
        sum_ref[here, :] = total
        parts, following = [zero, zero], []
        for n in range(16):
            state = jnp.exp2(rates[n] * step) * states[n] + coef_ref[n, token] * drive
            parts[n % 2] = parts[n % 2] + coef_ref[16 + n, token] * state
            following.append(state)
        y_ref[here, :] = parts[0] + parts[1]
        return total, tuple(following)

    total, states = lax.fori_loop(0, rows, advance, (zero, (zero,) * 16), unroll=4)
    packed = pack_state(states, total)
    for index in range(8):
        end_ref[index] = packed


def fold(ref, rates, limit, states, total):
    for position in range(8):
        more, step = unpack_state(ref, position)
        keep = position < limit
        states = [
            jnp.where(keep, jnp.exp2(rates[n] * step) * states[n] + more[n], states[n])
            for n in range(16)
        ]
        total = jnp.where(keep, total + step, total)
    return states, total


def group_kernel(mine_ref, got_ref, rate_ref, before_ref, step_ref, all_ref):
    rates = [rate_ref[n * 8 : n * 8 + 8, :] for n in range(16)]
    zero = jnp.zeros((8, 128), F32)
    states, total = fold(got_ref, rates, mine_ref[0], [zero] * 16, zero)
    for n in range(16):
        before_ref[n * 8 : n * 8 + 8, :] = states[n]
    step_ref[...] = total
    states, total = fold(got_ref, rates, 8, [zero] * 16, zero)
    packed = pack_state(states, total)
    for index in range(8):
        all_ref[index] = packed


def finish_kernel(
    mine_ref,
    coef_ref,
    got_ref,
    rate_ref,
    before_ref,
    before_step_ref,
    y_ref,
    sum_ref,
    conv_ref,
    gain_ref,
    z_ref,
    out_ref,
    dense,
):
    rows, width = conv_ref.shape
    rates = [rate_ref[n * 8 : n * 8 + 8, :] for n in range(16)]
    zero = jnp.zeros((8, 128), F32)
    states, _ = fold(got_ref, rates, mine_ref[0], [zero] * 16, zero)
    states = [
        jnp.exp2(rates[n] * before_step_ref[...]) * states[n] + before_ref[n * 8 : n * 8 + 8, :]
        for n in range(16)
    ]

    def advance(token, carry):
        here = pl.ds(pl.multiple_of(token * 8, 8), 8)
        total = sum_ref[here, :]
        parts = [y_ref[here, :], zero]
        for n in range(16):
            parts[n % 2] = parts[n % 2] + coef_ref[16 + n, token] * (
                jnp.exp2(rates[n] * total) * states[n]
            )
        dense[here, :] = parts[0] + parts[1]
        return carry

    lax.fori_loop(0, rows, advance, 0, unroll=4)
    for index in range(width // 128):
        lanes = slice(index * 128, index * 128 + 128)
        value = dense[pl.ds(index, rows, stride=8), :]
        value = value + gain_ref[:, lanes] * conv_ref[:, lanes]
        out_ref[:, lanes] = (value * silu(z_ref[:, lanes].astype(F32))).astype(BF16)


def shards(
    inner_x,
    inner_z,
    step_raw,
    conv_weight,
    state_proj,
    step_bias,
    decay_log,
    skip_gain,
    moe_tokens,
    routes,
    gate_weight,
    up_weight,
):
    rows, width = inner_x.shape
    shards_of = lax.axis_size(SEQ)
    rim = lax.ppermute(inner_x[rows - 3 :], SEQ, [(i, i + 1) for i in range(shards_of - 1)])
    swap = [(0, 1), (1, 0)]
    features = moe_tokens.shape[1]
    placed = call(
        place_kernel,
        shape((32, 2 * CAP, features // 2), BF16),
        [WHOLE] * 2,
        [pltpu.VMEM((2 * CAP, features // 2), F32)],
        name="place",
        flops=1 << 28,
    )(routes.T, moe_tokens)
    arrived = lax.all_to_all(placed, ("exp", "x"), split_axis=0, concat_axis=0, tiled=True)
    dense = shape((rows * width // 128, 128), F32)
    conv, step, drive, rate, part = call(
        conv_kernel,
        (
            shape((rows, width), F32),
            dense,
            dense,
            shape((128, 128), F32),
            shape((8, 32, rows), F32),
        ),
        [WHOLE] * 7,
        [pltpu.VMEM((rows + 8, width), F32)],
        name="conv", flops=1 << 29,
    )(inner_x, rim, step_raw, conv_weight, state_proj.T, step_bias[None], decay_log)
    dense = shape((rows * width // 128, 128), F32)
    conv, step, drive, rate, part = call(
        conv_kernel,
        (
            shape((rows, width), F32),
            dense,
            dense,
            shape((128, 128), F32),
            shape((8, 32, rows), F32),
        ),
        [WHOLE] * 7,
        [pltpu.VMEM((rows + 8, width), F32)],
        name="conv", flops=1 << 29,
    )(inner_x, rim, step_raw, conv_weight, state_proj.T, step_bias[None], decay_log)
    weight = jnp.concatenate([gate_weight[0], up_weight[0]], axis=0)
    arrived, part = lax.optimization_barrier((arrived, part))
    block = call(
        assemble_kernel,
        shape((4 * CAP, 4096), BF16),
        [WHOLE],
        [pltpu.VMEM((4 * CAP, 4096), F32)],
        name="assemble",
        vmem=16,
        flops=1 << 28,
    )(arrived)
    onward = [(2 * z + c, 2 * ((z + 1 - 2 * c) % 8) + c) for z in range(8) for c in range(2)]

    def step_on(rows):
        return lax.ppermute(rows, ("z", "c"), onward)

    own, twin = [block, step_on(block)], [lax.ppermute(block, "c", swap)]
    twin[0], part = lax.optimization_barrier((twin[0], part))
    twin.append(step_on(twin[0]))
    coef = lax.all_to_all(part, "exp", split_axis=0, concat_axis=0, tiled=True)
    own[1], coef = lax.optimization_barrier((own[1], coef))
    coef = jnp.sum(coef, axis=0)
    packed = shape((8, 160, 128), BF16)
    local, sums, ends = call(
        scan_kernel, (dense, dense, packed), [SMEM] + [WHOLE] * 3, name="scan", flops=1 << 31
    )(coef, step, drive, rate)
    for _ in range(2):
        own.append(step_on(own[-1]))
        twin.append(step_on(twin[-1]))
    own.append(step_on(own[-1]))
    near = lax.all_to_all(ends, ("x", "c"), split_axis=0, concat_axis=0, tiled=True)
    place_in = lax.axis_index(("x", "c")).astype(jnp.int32).reshape(1)
    before, before_step, whole = call(
        group_kernel,
        (shape((128, 128), F32), shape((8, 128), F32), packed),
        [SMEM, WHOLE, WHOLE],
        name="group", vmem=16, flops=1 << 28,
    )(place_in, near, rate)
    far = lax.all_to_all(whole, "z", split_axis=0, concat_axis=0, tiled=True)
    layer = lax.axis_index("z").astype(jnp.int32).reshape(1)
    mixed = call(
        finish_kernel,
        shape((rows, width), BF16),
        [SMEM, SMEM] + [WHOLE] * 9,
        [pltpu.VMEM(dense.shape, F32)],
        name="finish", flops=1 << 31,
    )(layer, coef, far, rate, before, before_step, local, sums, conv, skip_gain[None], inner_z)

    weights = gate_weight[0], up_weight[0]
    *sent, _ = lax.optimization_barrier((*weights, ends))
    pairs = [[lax.ppermute(weight, "c", swap) for weight in sent], weights]
    other_early, mine_early = expand([block, own[1], twin[1], own[2], twin[2]], pairs, "expand_early")
    late = [own[3], twin[3], own[4]]
    (other_late,) = expand(late, pairs[:1], "expand_other")
    (mine_late,) = expand(late, pairs[1:], "expand_mine")
    others = [lax.ppermute(part, "c", swap) for part in (other_early, other_late)]
    here = jnp.stack([lax.axis_index("z"), lax.axis_index("c")]).astype(jnp.int32)
    hidden = call(
        order_kernel,
        shape((gate_weight.shape[1], 1280), BF16),
        [SMEM] + [WHOLE] * 4,
        name="order",
        flops=1 << 28,
    )(here, mine_early, mine_late, *others)[None]
    return mixed, hidden


def solution(mesh):
    fine = Mesh(mesh.devices.reshape(8, 4, 2, 8), ("z", "x", "c", "exp"))
    return jax.shard_map(
        shards,
        mesh=fine,
        in_specs=(
            P(SEQ, "exp"),
            P(SEQ, "exp"),
            P(SEQ, "exp"),
            P(None, "exp"),
            P("exp", None),
            P("exp"),
            P(None, "exp"),
            P("exp"),
            P(SEQ, "exp"),
            P(SEQ, None),
            P("exp", SEQ, None),
            P("exp", SEQ, None),
        ),
        out_specs=(P(SEQ, "exp"), P("exp", SEQ, None)),
        check_vma=False,
    )
```

profile of v0, /device:TPU:1, one launch (start us, length us, event | category | flops | bytes accessed | tf_op | source)
XLA Modules:
  0.0 137.2 jit_solution(3644676919020804459)
XLA Ops:
  0.6 2.1 %place.1 = bf16[32,40,256]{2,1,0:T(8,128)(2,1)} custom-call(s32[2,128]{1,0:T(2,128)} %bitcast.20, bf16[128,512]{1,0:T(8,128)(2,1)} %refs_1_.1), custom_call_target="tpu_custom_call" | custom-call | flops 268435456 | bytes 4194304 | tf_op jit(solution)/shard_map/place/pallas_call | solution.py:55
  2.8 10.5 %all-to-all-start = ((bf16[32,40,256]{2,1,0:T(8,128)(2,1)}), bf16[32,40,256]{2,1,0:T(8,128)(2,1)S(1)}, u32[]{:S(2)}, u32[]{:S(2)}) async-start(bf16[32,40,256]{2,1,0:T(8,128)(2,1)} %place.1), calls=%async_computation | async-start | bytes 1310720 | tf_op jit(solution)/shard_map/all_to_all | solution.py:383
  13.3 0.7 slice.3
  14.0 4.2 %collective-permute-start = (bf16[3,1024]{1,0:T(4,128)(2,1)S(1)}, bf16[3,1024]{1,0:T(4,128)(2,1)S(1)}, u32[]{:S(2)}, u32[]{:S(2)}) collective-permute-start(bf16[3,1024]{1,0:T(4,128)(2,1)S(1)} %slice.3), channel_id=1, source_target_pairs={{0,8},{8,16},{16,24},{24,32},{32,40},{40,48},{48,56},{56,64},{64,7... | collective-permute-start | bytes 18440 | tf_op jit(solution)/shard_map/ppermute | solution.py:372
  18.3 0.8 collective-permute-done.refs_1_
  19.0 0.0 copy-start.9
  19.0 0.6 copy-done.9
  19.6 3.8 %conv.1 = (f32[128,1024]{1,0:T(8,128)}, f32[1024,128]{1,0:T(8,128)}, f32[1024,128]{1,0:T(8,128)}, f32[128,128]{1,0:T(8,128)}, f32[8,32,128]{2,1,0:T(8,128)}) custom-call(bf16[128,1024]{1,0:T(8,128)(2,1)} %refs_0_.1, bf16[3,1024]{1,0:T(4,128)(2,1)} %copy-done.9, bf16[128,1024]{1,0:T(8,128)(2,1)} %refs_2_.1, f32[4,1024]{1,0:T(4,128)} %refs_3_.1, ...), custom_call_target="tpu_custom_call" | custom-call | flops 536870912 | bytes 4194304 | tf_op jit(solution)/shard_map/conv/pallas_call | solution.py:55
  23.4 8.6 %all-to-all-done.refs_0_ = bf16[32,40,256]{2,1,0:T(8,128)(2,1)S(1)} async-done(((bf16[32,40,256]{2,1,0:T(8,128)(2,1)}), bf16[32,40,256]{2,1,0:T(8,128)(2,1)S(1)}, u32[]{:S(2)}, u32[]{:S(2)}) %all-to-all-start) | async-done | bytes 655392 | tf_op jit(solution)/shard_map/all_to_all | solution.py:383
  32.0 0.6 assemble.1.refs_0_
  32.6 0.0 copy-start
  32.6 4.4 %collective-permute-start.2 = (bf16[80,4096]{1,0:T(8,128)(2,1)S(1)}, bf16[80,4096]{1,0:T(8,128)(2,1)}, u32[]{:S(2)}, u32[]{:S(2)}) collective-permute-start(bf16[80,4096]{1,0:T(8,128)(2,1)S(1)} %assemble.1.refs_0_), channel_id=1, source_target_pairs={{0,8},{8,0},{1,9},{9,1},{2,10},{10,2},{3,11},{11,3},{4,12},{12,4},... | collective-permute-start | bytes 1966088 | tf_op jit(solution)/shard_map/ppermute | solution.py:428
  37.0 10.7 %collective-permute-start.1 = (bf16[80,4096]{1,0:T(8,128)(2,1)S(1)}, bf16[80,4096]{1,0:T(8,128)(2,1)}, u32[]{:S(2)}, u32[]{:S(2)}) collective-permute-start(bf16[80,4096]{1,0:T(8,128)(2,1)S(1)} %assemble.1.refs_0_), channel_id=1, source_target_pairs={{0,64},{8,456},{64,128},{72,8},{128,192},{136,72},{192,256},{200,1... | collective-permute-start | bytes 1966088 | tf_op jit(solution)/shard_map/ppermute | solution.py:426
  47.6 0.0 collective-permute-done.2
  47.6 3.4 %all-to-all-start.1 = ((f32[8,32,128]{2,1,0:T(8,128)}), f32[8,32,128]{2,1,0:T(8,128)S(1)}, u32[]{:S(2)}, u32[]{:S(2)}) async-start(f32[8,32,128]{2,1,0:T(8,128)} %get-tuple-element.26), calls=%async_computation.1 | async-start | bytes 262144 | tf_op jit(solution)/shard_map/all_to_all | solution.py:431
  51.0 2.2 %collective-permute-start.3 = (bf16[80,4096]{1,0:T(8,128)(2,1)}, bf16[80,4096]{1,0:T(8,128)(2,1)}, u32[]{:S(2)}, u32[]{:S(2)}) collective-permute-start(bf16[80,4096]{1,0:T(8,128)(2,1)} %collective-permute-done.2), channel_id=1, source_target_pairs={{0,64},{8,456},{64,128},{72,8},{128,192},{136,72},{192,256},{200,1... | collective-permute-start | bytes 1966088 | tf_op jit(solution)/shard_map/ppermute | solution.py:426
  53.2 1.9 %collective-permute-done.1.refs_1_ = bf16[80,4096]{1,0:T(8,128)(2,1)} collective-permute-done((bf16[80,4096]{1,0:T(8,128)(2,1)S(1)}, bf16[80,4096]{1,0:T(8,128)(2,1)}, u32[]{:S(2)}, u32[]{:S(2)}) %collective-permute-start.1) | collective-permute-done | bytes 655392 | tf_op jit(solution)/shard_map/ppermute | solution.py:426
  55.1 3.7 %all-to-all-done.1 = f32[8,32,128]{2,1,0:T(8,128)S(1)} async-done(((f32[8,32,128]{2,1,0:T(8,128)}), f32[8,32,128]{2,1,0:T(8,128)S(1)}, u32[]{:S(2)}, u32[]{:S(2)}) %all-to-all-start.1) | async-done | bytes 131104 | tf_op jit(solution)/shard_map/all_to_all | solution.py:431
  58.9 2.9 %collective-permute-start.4 = (bf16[80,4096]{1,0:T(8,128)(2,1)}, bf16[80,4096]{1,0:T(8,128)(2,1)}, u32[]{:S(2)}, u32[]{:S(2)}) collective-permute-start(bf16[80,4096]{1,0:T(8,128)(2,1)} %collective-permute-done.1.refs_1_), channel_id=1, source_target_pairs={{0,64},{8,456},{64,128},{72,8},{128,192},{136,72},{192,256},{200,1... | collective-permute-start | bytes 1966088 | tf_op jit(solution)/shard_map/ppermute | solution.py:426
  61.8 0.6 reduce_sum.9.refs_0_.refs_1_
  62.4 0.0 copy-start.4
  62.4 7.0 %scan.1 = (f32[1024,128]{1,0:T(8,128)}, f32[1024,128]{1,0:T(8,128)}, bf16[8,160,128]{2,1,0:T(8,128)(2,1)}) custom-call(f32[32,128]{1,0:T(8,128)} %reduce_sum.9.refs_0_.refs_1_, f32[1024,128]{1,0:T(8,128)} %get-tuple-element.28.refs_1_, f32[1024,128]{1,0:T(8,128)} %get-tuple-element.29.refs_2_, f32[128,128]{1,0:T(8,128)} %get-tuple-element.30.refs_3_.refs_2_), custom_call_target="tpu_custom_call" | custom-call | flops 2147483648 | bytes 4194304 | tf_op jit(solution)/shard_map/scan/pallas_call | solution.py:55
  69.4 0.0 copy-done
  69.4 0.0 copy-done.4
  69.4 1.9 %collective-permute-start.6 = (bf16[192,4096]{1,0:T(8,128)(2,1)S(1)}, bf16[192,4096]{1,0:T(8,128)(2,1)S(1)}, u32[]{:S(2)}, u32[]{:S(2)}) collective-permute-start(bf16[192,4096]{1,0:T(8,128)(2,1)S(1)} %bitcast.12), channel_id=1, source_target_pairs={{0,8},{8,0},{1,9},{9,1},{2,10},{10,2},{3,11},{11,3},{4,12},{12,4},... | collective-permute-start | bytes 4718600 | tf_op jit(solution)/shard_map/ppermute | solution.py:462
  71.3 2.4 %collective-permute-start.7 = (bf16[192,4096]{1,0:T(8,128)(2,1)}, bf16[192,4096]{1,0:T(8,128)(2,1)}, u32[]{:S(2)}, u32[]{:S(2)}) collective-permute-start(bf16[192,4096]{1,0:T(8,128)(2,1)} %bitcast.13), channel_id=1, source_target_pairs={{0,8},{8,0},{1,9},{9,1},{2,10},{10,2},{3,11},{11,3},{4,12},{12,4},... | collective-permute-start | bytes 4718600 | tf_op jit(solution)/shard_map/ppermute | solution.py:462
  73.8 0.0 collective-permute-done.3.refs_2_
  73.8 2.8 %collective-permute-start.5 = (bf16[80,4096]{1,0:T(8,128)(2,1)}, bf16[80,4096]{1,0:T(8,128)(2,1)}, u32[]{:S(2)}, u32[]{:S(2)}) collective-permute-start(bf16[80,4096]{1,0:T(8,128)(2,1)} %collective-permute-done.3.refs_2_), channel_id=1, source_target_pairs={{0,64},{8,456},{64,128},{72,8},{128,192},{136,72},{192,256},{200,1... | collective-permute-start | bytes 1966088 | tf_op jit(solution)/shard_map/ppermute | solution.py:426
  76.6 0.0 collective-permute-done.4.refs_3_
  76.6 3.6 %collective-permute-start.8 = (bf16[80,4096]{1,0:T(8,128)(2,1)}, bf16[80,4096]{1,0:T(8,128)(2,1)}, u32[]{:S(2)}, u32[]{:S(2)}) collective-permute-start(bf16[80,4096]{1,0:T(8,128)(2,1)} %collective-permute-done.4.refs_3_), channel_id=1, source_target_pairs={{0,64},{8,456},{64,128},{72,8},{128,192},{136,72},{192,256},{200,1... | collective-permute-start | bytes 1966088 | tf_op jit(solution)/shard_map/ppermute | solution.py:426
  80.2 4.1 %all-to-all-start.2 = ((bf16[8,160,128]{2,1,0:T(8,128)(2,1)}), bf16[8,160,128]{2,1,0:T(8,128)(2,1)S(1)}, u32[]{:S(2)}, u32[]{:S(2)}) async-start(bf16[8,160,128]{2,1,0:T(8,128)(2,1)} %get-tuple-element.31), calls=%async_computation.2 | async-start | bytes 655360 | tf_op jit(solution)/shard_map/all_to_all | solution.py:442
  84.4 1.3 collective-permute-done.5.refs_4_
  85.7 3.7 %collective-permute-start.9 = (bf16[80,4096]{1,0:T(8,128)(2,1)}, bf16[80,4096]{1,0:T(8,128)(2,1)}, u32[]{:S(2)}, u32[]{:S(2)}) collective-permute-start(bf16[80,4096]{1,0:T(8,128)(2,1)} %collective-permute-done.5.refs_4_), channel_id=1, source_target_pairs={{0,64},{8,456},{64,128},{72,8},{128,192},{136,72},{192,256},{200,1... | collective-permute-start | bytes 1966088 | tf_op jit(solution)/shard_map/ppermute | solution.py:426
  89.4 3.3 %collective-permute-done.8.refs_0_ = bf16[80,4096]{1,0:T(8,128)(2,1)} collective-permute-done((bf16[80,4096]{1,0:T(8,128)(2,1)}, bf16[80,4096]{1,0:T(8,128)(2,1)}, u32[]{:S(2)}, u32[]{:S(2)}) %collective-permute-start.8) | collective-permute-done | bytes 655392 | tf_op jit(solution)/shard_map/ppermute | solution.py:426
  92.7 3.7 %collective-permute-start.10 = (bf16[80,4096]{1,0:T(8,128)(2,1)}, bf16[80,4096]{1,0:T(8,128)(2,1)}, u32[]{:S(2)}, u32[]{:S(2)}) collective-permute-start(bf16[80,4096]{1,0:T(8,128)(2,1)} %collective-permute-done.8.refs_0_), channel_id=1, source_target_pairs={{0,64},{8,456},{64,128},{72,8},{128,192},{136,72},{192,256},{200,1... | collective-permute-start | bytes 1966088 | tf_op jit(solution)/shard_map/ppermute | solution.py:426
  96.5 0.0 all-to-all-done.2.refs_1_
  96.5 0.0 copy-done.1
  96.5 1.3 group.1
  97.7 0.0 copy-start.2
  97.8 0.6 copy-done.2
  98.4 4.7 %all-to-all-start.3 = ((bf16[8,160,128]{2,1,0:T(8,128)(2,1)}), bf16[8,160,128]{2,1,0:T(8,128)(2,1)S(1)}, u32[]{:S(2)}, u32[]{:S(2)}) async-start(bf16[8,160,128]{2,1,0:T(8,128)(2,1)} %get-tuple-element.32), calls=%async_computation.3 | async-start | bytes 655360 | tf_op jit(solution)/shard_map/all_to_all | solution.py:450
  103.1 0.6 pad_add_fusion.refs_0_
  103.7 0.0 collective-permute-done.6.refs_5_.refs_3_
  103.7 0.0 collective-permute-done.7.refs_6_.refs_4_
  103.7 1.1 copy-done.5
  104.8 8.1 %expand_early.1 = (bf16[192,400]{1,0:T(8,128)(2,1)}, bf16[192,400]{1,0:T(8,128)(2,1)}) custom-call(bf16[80,4096]{1,0:T(8,128)(2,1)} %copy-done, bf16[80,4096]{1,0:T(8,128)(2,1)} %collective-permute-done.1.refs_1_, bf16[80,4096]{1,0:T(8,128)(2,1)} %collective-permute-done.3.refs_2_, bf16[80,4096]{1,0:T(8,128)(2,1)} %collective-permute-done.4.refs_3_, ...), custom_call_target="tpu_custom_call" | custom-call | flops 2516582400 | bytes 8388608 | tf_op jit(solution)/shard_map/expand_early/pallas_call | solution.py:147
  113.0 0.0 copy-done.3
  113.0 2.9 %collective-permute-start.11 = (bf16[192,400]{1,0:T(8,128)(2,1)}, bf16[192,400]{1,0:T(8,128)(2,1)S(1)}, u32[]{:S(2)}, u32[]{:S(2)}) collective-permute-start(bf16[192,400]{1,0:T(8,128)(2,1)} %get-tuple-element.43), channel_id=1, source_target_pairs={{0,8},{8,0},{1,9},{9,1},{2,10},{10,2},{3,11},{11,3},{4,12},{12,4},... | collective-permute-start | bytes 460808 | tf_op jit(solution)/shard_map/ppermute | solution.py:467
  115.9 0.0 collective-permute-done.9.refs_1_
  115.9 0.0 collective-permute-done.10.refs_2_
  115.9 4.1 %expand_other.1 = bf16[192,240]{1,0:T(8,128)(2,1)} custom-call(bf16[80,4096]{1,0:T(8,128)(2,1)} %collective-permute-done.8.refs_0_, bf16[80,4096]{1,0:T(8,128)(2,1)} %collective-permute-done.9.refs_1_, bf16[80,4096]{1,0:T(8,128)(2,1)} %collective-permute-done.10.refs_2_, bf16[192,4096]{1,0:T(8,128)(2,1)} %copy-done.5, ...), custom_call_target="tpu_custom_call" | custom-call | flops 754974720 | bytes 8388608 | tf_op jit(solution)/shard_map/expand_other/pallas_call | solution.py:147
  120.1 1.9 %collective-permute-start.12 = (bf16[192,240]{1,0:T(8,128)(2,1)}, bf16[192,240]{1,0:T(8,128)(2,1)S(1)}, u32[]{:S(2)}, u32[]{:S(2)}) collective-permute-start(bf16[192,240]{1,0:T(8,128)(2,1)} %expand_other.1), channel_id=1, source_target_pairs={{0,8},{8,0},{1,9},{9,1},{2,10},{10,2},{3,11},{11,3},{4,12},{12,4},... | collective-permute-start | bytes 276488 | tf_op jit(solution)/shard_map/ppermute | solution.py:467
  122.0 0.0 all-to-all-done.3.refs_2_
  122.0 0.0 copy-start.6
  122.0 0.7 copy-done.6
  122.8 5.7 %finish.1 = bf16[128,1024]{1,0:T(8,128)(2,1)} custom-call(s32[1]{0:T(128)} %bitcast.refs_0_, f32[32,128]{1,0:T(8,128)} %reduce_sum.9.refs_0_.refs_1_, bf16[8,160,128]{2,1,0:T(8,128)(2,1)} %copy-done.6, f32[128,128]{1,0:T(8,128)} %get-tuple-element.30.refs_3_.refs_2_, f32[128,128]{1,0:T(8,128)} %copy-done.2, f32[8,128]{1,0:T(8,128)} %copy-done.3, ...), custom_call_target="tpu_custom_call" | custom-call | flops 2147483648 | bytes 4194304 | tf_op jit(solution)/shard_map/finish/pallas_call | solution.py:55
  128.4 4.1 %expand_mine.1.refs_2_ = bf16[192,240]{1,0:T(8,128)(2,1)} custom-call(bf16[80,4096]{1,0:T(8,128)(2,1)} %collective-permute-done.8.refs_0_, bf16[80,4096]{1,0:T(8,128)(2,1)} %collective-permute-done.9.refs_1_, bf16[80,4096]{1,0:T(8,128)(2,1)} %collective-permute-done.10.refs_2_, bf16[192,4096]{1,0:T(8,128)(2,1)} %bitcast.11, bf16[192,4096]{1,0:T(8,128)(2,1)} %bitcast.15), custom_call_target="tpu_custom_call" | custom-call | flops 754974720 | bytes 8388608 | tf_op jit(solution)/shard_map/expand_mine/pallas_call | solution.py:147
  132.6 0.0 collective-permute-done.11.refs_3_
  132.6 0.0 copy-start.7
  132.6 0.0 collective-permute-done.12.refs_4_
  132.6 0.0 copy-start.8
  132.6 0.6 copy-done.7
  133.3 0.1 copy-done.8
  133.3 3.9 %order.1 = bf16[192,1280]{1,0:T(8,128)(2,1)} custom-call(s32[2]{0:T(128)} %pad_add_fusion.refs_0_, bf16[192,400]{1,0:T(8,128)(2,1)} %get-tuple-element.42.refs_1_, bf16[192,240]{1,0:T(8,128)(2,1)} %expand_mine.1.refs_2_, bf16[192,400]{1,0:T(8,128)(2,1)} %copy-done.7, bf16[192,240]{1,0:T(8,128)(2,1)} %copy-done.8), custom_call_target="tpu_custom_call" | custom-call | flops 268435456 | bytes 4194304 | tf_op jit(solution)/shard_map/order/pallas_call | solution.py:55
  (3 shorter events, 0.0 us)
Async XLA Ops:
  2.8 29.2 %all-to-all-start = ((bf16[32,40,256]{2,1,0:T(8,128)(2,1)}), bf16[32,40,256]{2,1,0:T(8,128)(2,1)S(1)}, u32[]{:S(2)}, u32[]{:S(2)}) async-start(bf16[32,40,256]{2,1,0:T(8,128)(2,1)} %place.1), calls=%async_computation | async-start | bytes 1310720 | tf_op jit(solution)/shard_map/all_to_all | solution.py:383
  14.0 5.0 %collective-permute-start = (bf16[3,1024]{1,0:T(4,128)(2,1)S(1)}, bf16[3,1024]{1,0:T(4,128)(2,1)S(1)}, u32[]{:S(2)}, u32[]{:S(2)}) collective-permute-start(bf16[3,1024]{1,0:T(4,128)(2,1)S(1)} %slice.3), channel_id=1, source_target_pairs={{0,8},{8,16},{16,24},{24,32},{32,40},{40,48},{48,56},{56,64},{64,7... | collective-permute-start | bytes 18440 | tf_op jit(solution)/shard_map/ppermute | solution.py:372
  19.0 0.6 copy-start.9
  32.6 36.8 %copy-start = (bf16[80,4096]{1,0:T(8,128)(2,1)}, bf16[80,4096]{1,0:T(8,128)(2,1)S(1)}, u32[]{:S(2)}) copy-start(bf16[80,4096]{1,0:T(8,128)(2,1)S(1)} %assemble.1.refs_0_) | copy-start | bytes 1966084
  32.6 15.1 %collective-permute-start.2 = (bf16[80,4096]{1,0:T(8,128)(2,1)S(1)}, bf16[80,4096]{1,0:T(8,128)(2,1)}, u32[]{:S(2)}, u32[]{:S(2)}) collective-permute-start(bf16[80,4096]{1,0:T(8,128)(2,1)S(1)} %assemble.1.refs_0_), channel_id=1, source_target_pairs={{0,8},{8,0},{1,9},{9,1},{2,10},{10,2},{3,11},{11,3},{4,12},{12,4},... | collective-permute-start | bytes 1966088 | tf_op jit(solution)/shard_map/ppermute | solution.py:428
  37.0 18.2 %collective-permute-start.1 = (bf16[80,4096]{1,0:T(8,128)(2,1)S(1)}, bf16[80,4096]{1,0:T(8,128)(2,1)}, u32[]{:S(2)}, u32[]{:S(2)}) collective-permute-start(bf16[80,4096]{1,0:T(8,128)(2,1)S(1)} %assemble.1.refs_0_), channel_id=1, source_target_pairs={{0,64},{8,456},{64,128},{72,8},{128,192},{136,72},{192,256},{200,1... | collective-permute-start | bytes 1966088 | tf_op jit(solution)/shard_map/ppermute | solution.py:426
  47.6 11.2 %all-to-all-start.1 = ((f32[8,32,128]{2,1,0:T(8,128)}), f32[8,32,128]{2,1,0:T(8,128)S(1)}, u32[]{:S(2)}, u32[]{:S(2)}) async-start(f32[8,32,128]{2,1,0:T(8,128)} %get-tuple-element.26), calls=%async_computation.1 | async-start | bytes 262144 | tf_op jit(solution)/shard_map/all_to_all | solution.py:431
  51.0 22.7 %collective-permute-start.3 = (bf16[80,4096]{1,0:T(8,128)(2,1)}, bf16[80,4096]{1,0:T(8,128)(2,1)}, u32[]{:S(2)}, u32[]{:S(2)}) collective-permute-start(bf16[80,4096]{1,0:T(8,128)(2,1)} %collective-permute-done.2), channel_id=1, source_target_pairs={{0,64},{8,456},{64,128},{72,8},{128,192},{136,72},{192,256},{200,1... | collective-permute-start | bytes 1966088 | tf_op jit(solution)/shard_map/ppermute | solution.py:426
  58.9 17.7 %collective-permute-start.4 = (bf16[80,4096]{1,0:T(8,128)(2,1)}, bf16[80,4096]{1,0:T(8,128)(2,1)}, u32[]{:S(2)}, u32[]{:S(2)}) collective-permute-start(bf16[80,4096]{1,0:T(8,128)(2,1)} %collective-permute-done.1.refs_1_), channel_id=1, source_target_pairs={{0,64},{8,456},{64,128},{72,8},{128,192},{136,72},{192,256},{200,1... | collective-permute-start | bytes 1966088 | tf_op jit(solution)/shard_map/ppermute | solution.py:426
  62.4 7.0 %copy-start.4 = (bf16[1,192,4096]{2,1,0:T(8,128)(2,1)S(1)}, bf16[1,192,4096]{2,1,0:T(8,128)(2,1)}, u32[]{:S(2)}) copy-start(bf16[1,192,4096]{2,1,0:T(8,128)(2,1)} %param.22) | copy-start | bytes 4718596
  62.4 34.1 %copy-start.1 = (f32[128,128]{1,0:T(8,128)S(1)}, f32[128,128]{1,0:T(8,128)}, u32[]{:S(2)}) copy-start(f32[128,128]{1,0:T(8,128)} %get-tuple-element.30.refs_3_.refs_2_) | copy-start | bytes 196612
  69.4 34.3 %collective-permute-start.6 = (bf16[192,4096]{1,0:T(8,128)(2,1)S(1)}, bf16[192,4096]{1,0:T(8,128)(2,1)S(1)}, u32[]{:S(2)}, u32[]{:S(2)}) collective-permute-start(bf16[192,4096]{1,0:T(8,128)(2,1)S(1)} %bitcast.12), channel_id=1, source_target_pairs={{0,8},{8,0},{1,9},{9,1},{2,10},{10,2},{3,11},{11,3},{4,12},{12,4},... | collective-permute-start | bytes 4718600 | tf_op jit(solution)/shard_map/ppermute | solution.py:462
  71.3 32.4 %collective-permute-start.7 = (bf16[192,4096]{1,0:T(8,128)(2,1)}, bf16[192,4096]{1,0:T(8,128)(2,1)}, u32[]{:S(2)}, u32[]{:S(2)}) collective-permute-start(bf16[192,4096]{1,0:T(8,128)(2,1)} %bitcast.13), channel_id=1, source_target_pairs={{0,8},{8,0},{1,9},{9,1},{2,10},{10,2},{3,11},{11,3},{4,12},{12,4},... | collective-permute-start | bytes 4718600 | tf_op jit(solution)/shard_map/ppermute | solution.py:462
  73.8 11.9 %collective-permute-start.5 = (bf16[80,4096]{1,0:T(8,128)(2,1)}, bf16[80,4096]{1,0:T(8,128)(2,1)}, u32[]{:S(2)}, u32[]{:S(2)}) collective-permute-start(bf16[80,4096]{1,0:T(8,128)(2,1)} %collective-permute-done.3.refs_2_), channel_id=1, source_target_pairs={{0,64},{8,456},{64,128},{72,8},{128,192},{136,72},{192,256},{200,1... | collective-permute-start | bytes 1966088 | tf_op jit(solution)/shard_map/ppermute | solution.py:426
  76.6 16.1 %collective-permute-start.8 = (bf16[80,4096]{1,0:T(8,128)(2,1)}, bf16[80,4096]{1,0:T(8,128)(2,1)}, u32[]{:S(2)}, u32[]{:S(2)}) collective-permute-start(bf16[80,4096]{1,0:T(8,128)(2,1)} %collective-permute-done.4.refs_3_), channel_id=1, source_target_pairs={{0,64},{8,456},{64,128},{72,8},{128,192},{136,72},{192,256},{200,1... | collective-permute-start | bytes 1966088 | tf_op jit(solution)/shard_map/ppermute | solution.py:426
  80.2 16.2 %all-to-all-start.2 = ((bf16[8,160,128]{2,1,0:T(8,128)(2,1)}), bf16[8,160,128]{2,1,0:T(8,128)(2,1)S(1)}, u32[]{:S(2)}, u32[]{:S(2)}) async-start(bf16[8,160,128]{2,1,0:T(8,128)(2,1)} %get-tuple-element.31), calls=%async_computation.2 | async-start | bytes 655360 | tf_op jit(solution)/shard_map/all_to_all | solution.py:442
  85.7 30.2 %collective-permute-start.9 = (bf16[80,4096]{1,0:T(8,128)(2,1)}, bf16[80,4096]{1,0:T(8,128)(2,1)}, u32[]{:S(2)}, u32[]{:S(2)}) collective-permute-start(bf16[80,4096]{1,0:T(8,128)(2,1)} %collective-permute-done.5.refs_4_), channel_id=1, source_target_pairs={{0,64},{8,456},{64,128},{72,8},{128,192},{136,72},{192,256},{200,1... | collective-permute-start | bytes 1966088 | tf_op jit(solution)/shard_map/ppermute | solution.py:426
  92.7 23.2 %collective-permute-start.10 = (bf16[80,4096]{1,0:T(8,128)(2,1)}, bf16[80,4096]{1,0:T(8,128)(2,1)}, u32[]{:S(2)}, u32[]{:S(2)}) collective-permute-start(bf16[80,4096]{1,0:T(8,128)(2,1)} %collective-permute-done.8.refs_0_), channel_id=1, source_target_pairs={{0,64},{8,456},{64,128},{72,8},{128,192},{136,72},{192,256},{200,1... | collective-permute-start | bytes 1966088 | tf_op jit(solution)/shard_map/ppermute | solution.py:426
  97.7 0.6 copy-start.2
  98.4 14.6 %copy-start.3 = (f32[8,128]{1,0:T(8,128)}, f32[8,128]{1,0:T(8,128)S(1)}, u32[]{:S(2)}) copy-start(f32[8,128]{1,0:T(8,128)S(1)} %get-tuple-element.34.refs_5_) | copy-start | bytes 12292
  98.4 23.7 %all-to-all-start.3 = ((bf16[8,160,128]{2,1,0:T(8,128)(2,1)}), bf16[8,160,128]{2,1,0:T(8,128)(2,1)S(1)}, u32[]{:S(2)}, u32[]{:S(2)}) async-start(bf16[8,160,128]{2,1,0:T(8,128)(2,1)} %get-tuple-element.32), calls=%async_computation.3 | async-start | bytes 655360 | tf_op jit(solution)/shard_map/all_to_all | solution.py:450
  103.7 1.1 copy-start.5
  113.0 19.6 %collective-permute-start.11 = (bf16[192,400]{1,0:T(8,128)(2,1)}, bf16[192,400]{1,0:T(8,128)(2,1)S(1)}, u32[]{:S(2)}, u32[]{:S(2)}) collective-permute-start(bf16[192,400]{1,0:T(8,128)(2,1)} %get-tuple-element.43), channel_id=1, source_target_pairs={{0,8},{8,0},{1,9},{9,1},{2,10},{10,2},{3,11},{11,3},{4,12},{12,4},... | collective-permute-start | bytes 460808 | tf_op jit(solution)/shard_map/ppermute | solution.py:467
  120.1 12.5 %collective-permute-start.12 = (bf16[192,240]{1,0:T(8,128)(2,1)}, bf16[192,240]{1,0:T(8,128)(2,1)S(1)}, u32[]{:S(2)}, u32[]{:S(2)}) collective-permute-start(bf16[192,240]{1,0:T(8,128)(2,1)} %expand_other.1), channel_id=1, source_target_pairs={{0,8},{8,0},{1,9},{9,1},{2,10},{10,2},{3,11},{11,3},{4,12},{12,4},... | collective-permute-start | bytes 276488 | tf_op jit(solution)/shard_map/ppermute | solution.py:467
  122.0 0.7 copy-start.6
  132.6 0.7 copy-start.7
  132.6 0.7 copy-start.8
where the time goes:
time: 138 us; the launch traced here: 137 us
  starting transfers between devices  70.1 us (51%)
  Pallas kernels  40.7 us (29%)
  waiting for transfers between devices  19.6 us (14%)
  local copies, waits for them, and re-layouts  4.53 us (3%)
    ppermute x7, starting transfers between devices, step_on(): return lax.ppermute(rows, ('z', 'c'), onward)  29.6 us
    pallas_call x7, Pallas kernels, run(): pl.pallas_call(body, out_shape=outs, in_specs=in_specs, out_specs=(WHOLE,...  24.3 us
    pallas_call x3, Pallas kernels, expand(): pl.pallas_call(functools.partial(expand_kernel, len(blocks), total), out_...  16.4 us
    all_to_all x1, starting transfers between devices, shards(): lax.all_to_all(placed, ('exp', 'x'), split_axis=0, concat_axis=0, tiled=T...  10.5 us
    all_to_all x1, waiting for transfers between devices, shards(): lax.all_to_all(placed, ('exp', 'x'), split_axis=0, concat_axis=0, tiled=T...  8.56 us
    ppermute x7, waiting for transfers between devices, step_on(): return lax.ppermute(rows, ('z', 'c'), onward)  6.56 us
    ppermute x2, starting transfers between devices, shards(): lax.ppermute(part, 'c', swap)  4.83 us
    all_to_all x1, starting transfers between devices, shards(): far = lax.all_to_all(whole, 'z', split_axis=0, concat_axis=0, tiled=True)  4.7 us
  transfers between devices with their start and end apart: 17, of which 6 were waited for; matrix products, arithmetic and copies ran while one was open for 1% of the time, Pallas kernels for 25%

commit v1 on v0

--- a/solution.py
+++ b/solution.py
@@ -121,7 +121,7 @@
         pltpu.make_async_copy(source, target, sems.at[index])
         for index, (source, target) in enumerate(copies)
     ]
-    for copy in copies[blocks:] + copies[:blocks]:
+    for copy in copies:
         copy.start()
     for copy in copies[:blocks]:
         copy.wait()
@@ -171,9 +171,26 @@
 LATE = ((3, 0), (3, 1), (4, 0))
 
 
-def order_kernel(place_ref, mine_early, mine_late, other_early, other_late, out_ref):
-    columns = out_ref.shape[1]
-    total = jnp.zeros(out_ref.shape, F32)
+def last_kernel(place_ref, *refs):
+    (*sources, out_ref), held = refs[:9], refs[9:-1]
+    rows, weight, mine_early, other_early, other_late, mine_late, out, sems = *held, refs[-1]
+    size, units = sources[0].shape[0], sources[3].shape[0]
+    targets = [rows.at[pl.ds(index * size, size)] for index in range(3)]
+    targets += [weight.at[pl.ds(index * units, units)] for index in range(2)]
+    targets += [mine_early, other_early, other_late]
+    copies = [
+        pltpu.make_async_copy(source, target, sems.at[index])
+        for index, (source, target) in enumerate(zip(sources, targets))
+    ]
+    for copy in copies:
+        copy.start()
+    for copy in copies:
+        copy.wait()
+    both = lax.dot_general(
+        weight[...], rows[...], (((1,), (1,)), ((), ())), preferred_element_type=F32
+    )
+    mine_late[...] = (silu(both[:units]) * both[units:]).astype(BF16)
+    places = []
     for pair, blocks in (((mine_early, other_early), EARLY), ((mine_late, other_late), LATE)):
         count = pair[0].shape[1]
         row = lax.broadcasted_iota(jnp.int32, (count, 1), 0)
@@ -184,14 +201,44 @@
             steps = jnp.where(block == index, step, steps)
             twin = jnp.where(block == index, other, twin)
         base = within + divided(within, CAP) * CAP
-        column = lax.broadcasted_iota(jnp.int32, (count, columns), 1)
         for ref, holder in zip(pair, (place_ref[1], 1 - place_ref[1])):
             layer = (place_ref[0] + steps * (2 * holder - 1)) & 7
             core = holder + twin * (1 - 2 * holder)
-            target = layer * (8 * CAP) + core * CAP + base
+            places.append((ref, layer * (8 * CAP) + core * CAP + base))
+    for start in range(0, out.shape[1], 256):
+        total = jnp.zeros((units, 256), F32)
+        for ref, target in places:
+            column = lax.broadcasted_iota(jnp.int32, (ref.shape[1], 256), 1) + start
             table = jnp.where(column == target, 1.0, 0.0).astype(BF16)
             total = total + jnp.dot(ref[...], table, preferred_element_type=F32)
-    out_ref[...] = total.astype(BF16)
+        out[:, start : start + 256] = total.astype(BF16)
+    copy = pltpu.make_async_copy(out, out_ref, sems.at[0])
+    copy.start()
+    copy.wait()
+
+
+def last(place, blocks, pair, mine_early, other_early, other_late):
+    units, count = pair[0].shape[0], 3 * blocks[0].shape[0]
+    out = shape((units, 1280), BF16)
+    return pl.pallas_call(
+        last_kernel,
+        out_shape=out,
+        in_specs=[SMEM] + [WHOLE] * 8,
+        out_specs=WHOLE,
+        scratch_shapes=[
+            pltpu.VMEM((count, 4096), BF16),
+            pltpu.VMEM((2 * units, 4096), BF16),
+            pltpu.VMEM(mine_early.shape, BF16),
+            pltpu.VMEM(other_early.shape, BF16),
+            pltpu.VMEM((units, count), BF16),
+            pltpu.VMEM((units, count), BF16),
+            pltpu.VMEM(out.shape, BF16),
+            pltpu.SemaphoreType.DMA((8,)),
+        ],
+        name="last",
+        compiler_params=pltpu.CompilerParams(vmem_limit_bytes=60 << 20),
+        cost_estimate=pl.CostEstimate(flops=1 << 30, transcendentals=0, bytes_accessed=8 << 20),
+    )(place, *blocks, *pair, mine_early, other_early, other_late)
 
 
 def silu(value):
@@ -410,7 +457,10 @@
         name="conv", flops=1 << 29,
     )(inner_x, rim, step_raw, conv_weight, state_proj.T, step_bias[None], decay_log)
     weight = jnp.concatenate([gate_weight[0], up_weight[0]], axis=0)
-    arrived, part = lax.optimization_barrier((arrived, part))
+    weights = gate_weight[0], up_weight[0]
+    others = [lax.ppermute(weight, "c", swap) for weight in weights]
+    arrived, part, *others = lax.optimization_barrier((arrived, part, *others))
+    pairs = [others, weights]
     block = call(
         assemble_kernel,
         shape((4 * CAP, 4096), BF16),
@@ -435,10 +485,12 @@
     local, sums, ends = call(
         scan_kernel, (dense, dense, packed), [SMEM] + [WHOLE] * 3, name="scan", flops=1 << 31
     )(coef, step, drive, rate)
-    for _ in range(2):
-        own.append(step_on(own[-1]))
-        twin.append(step_on(twin[-1]))
-    own.append(step_on(own[-1]))
+    own.append(step_on(own[1]))
+    twin.append(step_on(twin[1]))
+    own[2], _ = lax.optimization_barrier((own[2], ends))
+    own.append(step_on(own[2]))
+    twin.append(step_on(twin[2]))
+    own.append(step_on(own[3]))
     near = lax.all_to_all(ends, ("x", "c"), split_axis=0, concat_axis=0, tiled=True)
     place_in = lax.axis_index(("x", "c")).astype(jnp.int32).reshape(1)
     before, before_step, whole = call(
@@ -457,22 +509,13 @@
         name="finish", flops=1 << 31,
     )(layer, coef, far, rate, before, before_step, local, sums, conv, skip_gain[None], inner_z)
 
-    weights = gate_weight[0], up_weight[0]
-    *sent, _ = lax.optimization_barrier((*weights, ends))
-    pairs = [[lax.ppermute(weight, "c", swap) for weight in sent], weights]
     other_early, mine_early = expand([block, own[1], twin[1], own[2], twin[2]], pairs, "expand_early")
     late = [own[3], twin[3], own[4]]
     (other_late,) = expand(late, pairs[:1], "expand_other")
-    (mine_late,) = expand(late, pairs[1:], "expand_mine")
-    others = [lax.ppermute(part, "c", swap) for part in (other_early, other_late)]
+    other_early, other_late = (lax.ppermute(part, "c", swap) for part in (other_early, other_late))
     here = jnp.stack([lax.axis_index("z"), lax.axis_index("c")]).astype(jnp.int32)
-    hidden = call(
-        order_kernel,
-        shape((gate_weight.shape[1], 1280), BF16),
-        [SMEM] + [WHOLE] * 4,
-        name="order",
-        flops=1 << 28,
-    )(here, mine_early, mine_late, *others)[None]
+    other_late, mixed = lax.optimization_barrier((other_late, mixed))
+    hidden = last(here, late, weights, mine_early, other_early, other_late)[None]
     return mixed, hidden
 
 

time: 138 us -> 138 us (level)
  waiting for transfers between devices: 19.6 us -> 21.3 us
  Pallas kernels: 40.7 us -> 39.2 us
  starting transfers between devices: 70.1 us -> 68.6 us
    pallas_call x0 -> x1, Pallas kernels: none -> 7.33 us  [last(): pl.pallas_call(last_kernel, out_shape=out, in_specs=[SMEM] + [WHOLE] * 8,...]
    ppermute x2, starting transfers between devices: 4.33 us -> 10.7 us  [shards(): others = [lax.ppermute(weight, 'c', swap) for weight in weights]]
    all_to_all x1, starting transfers between devices: 10.5 us -> 4.31 us  [shards(): lax.all_to_all(placed, ('exp', 'x'), split_axis=0, concat_axis=0, tiled=T...]
    pallas_call x3 -> x2, Pallas kernels: 16.4 us -> 11.5 us  [expand(): pl.pallas_call(functools.partial(expand_kernel, len(blocks), total), out_...]
    pallas_call x7 -> x6, Pallas kernels: 24.3 us -> 20.4 us  [run(): pl.pallas_call(body, out_shape=outs, in_specs=in_specs, out_specs=(WHOLE,...]
    ppermute x7, starting transfers between devices: 29.6 us -> 26.3 us  [step_on(): return lax.ppermute(rows, ('z', 'c'), onward)]
    ppermute x2, starting transfers between devices: 4.83 us -> 6.89 us  [shards(): lax.ppermute(part, 'c', swap)]
    ppermute x7, waiting for transfers between devices: 6.56 us -> 8.08 us  [step_on(): return lax.ppermute(rows, ('z', 'c'), onward)]
  transfers between devices with their start and end apart: 17 -> 17, of which waited for: 6 -> 6; matrix products, arithmetic and copies ran while one was open for 1% -> 1% of each run, Pallas kernels for 25% -> 23%
where the time goes in v1:
time: 138 us; the launch traced here: 136 us
  starting transfers between devices  68.6 us (50%)
  Pallas kernels  39.2 us (28%)
  waiting for transfers between devices  21.3 us (15%)
  local copies, waits for them, and re-layouts  5.04 us (4%)
    ppermute x7, starting transfers between devices, step_on(): return lax.ppermute(rows, ('z', 'c'), onward)  26.3 us
    pallas_call x6, Pallas kernels, run(): pl.pallas_call(body, out_shape=outs, in_specs=in_specs, out_specs=(WHOLE,...  20.4 us
    pallas_call x2, Pallas kernels, expand(): pl.pallas_call(functools.partial(expand_kernel, len(blocks), total), out_...  11.5 us
    ppermute x2, starting transfers between devices, shards(): others = [lax.ppermute(weight, 'c', swap) for weight in weights]  10.7 us
    all_to_all x1, waiting for transfers between devices, shards(): lax.all_to_all(placed, ('exp', 'x'), split_axis=0, concat_axis=0, tiled=T...  8.68 us
    ppermute x7, waiting for transfers between devices, step_on(): return lax.ppermute(rows, ('z', 'c'), onward)  8.08 us
    pallas_call x1, Pallas kernels, last(): pl.pallas_call(last_kernel, out_shape=out, in_specs=[SMEM] + [WHOLE] * 8,...  7.33 us
    ppermute x2, starting transfers between devices, shards(): lax.ppermute(part, 'c', swap)  6.89 us
  transfers between devices with their start and end apart: 17, of which 6 were waited for; matrix products, arithmetic and copies ran while one was open for 1% of the time, Pallas kernels for 23%

profile of v1, /device:TPU:1, one launch (start us, length us, event | category | flops | bytes accessed | tf_op | source)
XLA Modules:
  0.0 136.4 jit_solution(8637708222214221450)
XLA Ops:
  0.6 8.8 %collective-permute-start.1 = (bf16[192,4096]{1,0:T(8,128)(2,1)}, bf16[192,4096]{1,0:T(8,128)(2,1)S(1)}, u32[]{:S(2)}, u32[]{:S(2)}) collective-permute-start(bf16[192,4096]{1,0:T(8,128)(2,1)} %bitcast.10), channel_id=1, source_target_pairs={{0,8},{8,0},{1,9},{9,1},{2,10},{10,2},{3,11},{11,3},{4,12},{12,4},... | collective-permute-start | bytes 4718600 | tf_op jit(solution)/shard_map/ppermute | solution.py:461
  9.4 1.9 %collective-permute-start.2 = (bf16[192,4096]{1,0:T(8,128)(2,1)}, bf16[192,4096]{1,0:T(8,128)(2,1)}, u32[]{:S(2)}, u32[]{:S(2)}) collective-permute-start(bf16[192,4096]{1,0:T(8,128)(2,1)} %bitcast.13), channel_id=1, source_target_pairs={{0,8},{8,0},{1,9},{9,1},{2,10},{10,2},{3,11},{11,3},{4,12},{12,4},... | collective-permute-start | bytes 4718600 | tf_op jit(solution)/shard_map/ppermute | solution.py:461
  11.4 2.1 %place.1 = bf16[32,40,256]{2,1,0:T(8,128)(2,1)} custom-call(s32[2,128]{1,0:T(2,128)} %bitcast.20, bf16[128,512]{1,0:T(8,128)(2,1)} %refs_1_.1), custom_call_target="tpu_custom_call" | custom-call | flops 268435456 | bytes 4194304 | tf_op jit(solution)/shard_map/place/pallas_call | solution.py:55
  13.5 4.3 %all-to-all-start = ((bf16[32,40,256]{2,1,0:T(8,128)(2,1)}), bf16[32,40,256]{2,1,0:T(8,128)(2,1)S(1)}, u32[]{:S(2)}, u32[]{:S(2)}) async-start(bf16[32,40,256]{2,1,0:T(8,128)(2,1)} %place.1), calls=%async_computation | async-start | bytes 1310720 | tf_op jit(solution)/shard_map/all_to_all | solution.py:430
  17.8 0.7 slice.3
  18.5 4.1 %collective-permute-start = (bf16[3,1024]{1,0:T(4,128)(2,1)S(1)}, bf16[3,1024]{1,0:T(4,128)(2,1)S(1)}, u32[]{:S(2)}, u32[]{:S(2)}) collective-permute-start(bf16[3,1024]{1,0:T(4,128)(2,1)S(1)} %slice.3), channel_id=1, source_target_pairs={{0,8},{8,16},{16,24},{24,32},{32,40},{40,48},{48,56},{56,64},{64,7... | collective-permute-start | bytes 18440 | tf_op jit(solution)/shard_map/ppermute | solution.py:419
  22.6 0.8 collective-permute-done.refs_1_
  23.4 0.6 copy-done.12
  24.0 3.8 %conv.1 = (f32[128,1024]{1,0:T(8,128)}, f32[1024,128]{1,0:T(8,128)}, f32[1024,128]{1,0:T(8,128)}, f32[128,128]{1,0:T(8,128)}, f32[8,32,128]{2,1,0:T(8,128)}) custom-call(bf16[128,1024]{1,0:T(8,128)(2,1)} %refs_0_.1, bf16[3,1024]{1,0:T(4,128)(2,1)} %copy-done.12, bf16[128,1024]{1,0:T(8,128)(2,1)} %refs_2_.1, f32[4,1024]{1,0:T(4,128)} %refs_3_.1, ...), custom_call_target="tpu_custom_call" | custom-call | flops 536870912 | bytes 4194304 | tf_op jit(solution)/shard_map/conv/pallas_call | solution.py:55
  27.8 8.7 %all-to-all-done.refs_0_ = bf16[32,40,256]{2,1,0:T(8,128)(2,1)S(1)} async-done(((bf16[32,40,256]{2,1,0:T(8,128)(2,1)}), bf16[32,40,256]{2,1,0:T(8,128)(2,1)S(1)}, u32[]{:S(2)}, u32[]{:S(2)}) %all-to-all-start) | async-done | bytes 655392 | tf_op jit(solution)/shard_map/all_to_all | solution.py:430
  36.5 0.0 collective-permute-done.1.refs_3_.refs_5_
  36.5 0.0 collective-permute-done.2.refs_4_.refs_6_
  36.5 0.6 assemble.1.refs_0_
  37.1 0.0 copy-start
  37.1 4.5 %collective-permute-start.4 = (bf16[80,4096]{1,0:T(8,128)(2,1)S(1)}, bf16[80,4096]{1,0:T(8,128)(2,1)}, u32[]{:S(2)}, u32[]{:S(2)}) collective-permute-start(bf16[80,4096]{1,0:T(8,128)(2,1)S(1)} %assemble.1.refs_0_), channel_id=1, source_target_pairs={{0,8},{8,0},{1,9},{9,1},{2,10},{10,2},{3,11},{11,3},{4,12},{12,4},... | collective-permute-start | bytes 1966088 | tf_op jit(solution)/shard_map/ppermute | solution.py:478
  41.6 10.7 %collective-permute-start.3 = (bf16[80,4096]{1,0:T(8,128)(2,1)S(1)}, bf16[80,4096]{1,0:T(8,128)(2,1)S(1)}, u32[]{:S(2)}, u32[]{:S(2)}) collective-permute-start(bf16[80,4096]{1,0:T(8,128)(2,1)S(1)} %assemble.1.refs_0_), channel_id=1, source_target_pairs={{0,64},{8,456},{64,128},{72,8},{128,192},{136,72},{192,256},{200,1... | collective-permute-start | bytes 1966088 | tf_op jit(solution)/shard_map/ppermute | solution.py:476
  52.3 0.0 collective-permute-done.4
  52.3 3.4 %all-to-all-start.1 = ((f32[8,32,128]{2,1,0:T(8,128)}), f32[8,32,128]{2,1,0:T(8,128)S(1)}, u32[]{:S(2)}, u32[]{:S(2)}) async-start(f32[8,32,128]{2,1,0:T(8,128)} %get-tuple-element.29), calls=%async_computation.1 | async-start | bytes 262144 | tf_op jit(solution)/shard_map/all_to_all | solution.py:481
  55.7 2.2 %collective-permute-start.7 = (bf16[80,4096]{1,0:T(8,128)(2,1)}, bf16[80,4096]{1,0:T(8,128)(2,1)}, u32[]{:S(2)}, u32[]{:S(2)}) collective-permute-start(bf16[80,4096]{1,0:T(8,128)(2,1)} %collective-permute-done.4), channel_id=1, source_target_pairs={{0,64},{8,456},{64,128},{72,8},{128,192},{136,72},{192,256},{200,1... | collective-permute-start | bytes 1966088 | tf_op jit(solution)/shard_map/ppermute | solution.py:476
  57.9 1.9 %collective-permute-done.3.refs_1_ = bf16[80,4096]{1,0:T(8,128)(2,1)S(1)} collective-permute-done((bf16[80,4096]{1,0:T(8,128)(2,1)S(1)}, bf16[80,4096]{1,0:T(8,128)(2,1)S(1)}, u32[]{:S(2)}, u32[]{:S(2)}) %collective-permute-start.3) | collective-permute-done | bytes 655392 | tf_op jit(solution)/shard_map/ppermute | solution.py:476
  59.8 3.7 %all-to-all-done.1 = f32[8,32,128]{2,1,0:T(8,128)S(1)} async-done(((f32[8,32,128]{2,1,0:T(8,128)}), f32[8,32,128]{2,1,0:T(8,128)S(1)}, u32[]{:S(2)}, u32[]{:S(2)}) %all-to-all-start.1) | async-done | bytes 131104 | tf_op jit(solution)/shard_map/all_to_all | solution.py:481
  63.5 2.9 %collective-permute-start.5 = (bf16[80,4096]{1,0:T(8,128)(2,1)S(1)}, bf16[80,4096]{1,0:T(8,128)(2,1)}, u32[]{:S(2)}, u32[]{:S(2)}) collective-permute-start(bf16[80,4096]{1,0:T(8,128)(2,1)S(1)} %collective-permute-done.3.refs_1_), channel_id=1, source_target_pairs={{0,64},{8,456},{64,128},{72,8},{128,192},{136,72},{192,256},{200,1... | collective-permute-start | bytes 1966088 | tf_op jit(solution)/shard_map/ppermute | solution.py:476
  66.4 0.6 reduce_sum.9.refs_0_.refs_1_
  67.0 7.0 %scan.1 = (f32[1024,128]{1,0:T(8,128)}, f32[1024,128]{1,0:T(8,128)}, bf16[8,160,128]{2,1,0:T(8,128)(2,1)}) custom-call(f32[32,128]{1,0:T(8,128)} %reduce_sum.9.refs_0_.refs_1_, f32[1024,128]{1,0:T(8,128)} %get-tuple-element.32.refs_1_, f32[1024,128]{1,0:T(8,128)} %get-tuple-element.33.refs_2_, f32[128,128]{1,0:T(8,128)} %get-tuple-element.34.refs_3_.refs_2_), custom_call_target="tpu_custom_call" | custom-call | flops 2147483648 | bytes 4194304 | tf_op jit(solution)/shard_map/scan/pallas_call | solution.py:55
  74.0 0.0 copy-done.4
  74.1 0.0 copy-done
  74.1 0.0 copy-done.8
  74.1 0.0 collective-permute-done.7.refs_2_
  74.1 1.9 %collective-permute-start.8 = (bf16[80,4096]{1,0:T(8,128)(2,1)}, bf16[80,4096]{1,0:T(8,128)(2,1)}, u32[]{:S(2)}, u32[]{:S(2)}) collective-permute-start(bf16[80,4096]{1,0:T(8,128)(2,1)} %collective-permute-done.7.refs_2_), channel_id=1, source_target_pairs={{0,64},{8,456},{64,128},{72,8},{128,192},{136,72},{192,256},{200,1... | collective-permute-start | bytes 1966088 | tf_op jit(solution)/shard_map/ppermute | solution.py:476
  76.0 0.0 collective-permute-done.5.refs_3_
  76.0 3.0 %collective-permute-start.6 = (bf16[80,4096]{1,0:T(8,128)(2,1)}, bf16[80,4096]{1,0:T(8,128)(2,1)S(1)}, u32[]{:S(2)}, u32[]{:S(2)}) collective-permute-start(bf16[80,4096]{1,0:T(8,128)(2,1)} %collective-permute-done.5.refs_3_), channel_id=1, source_target_pairs={{0,64},{8,456},{64,128},{72,8},{128,192},{136,72},{192,256},{200,1... | collective-permute-start | bytes 1966088 | tf_op jit(solution)/shard_map/ppermute | solution.py:476
  79.1 4.9 %all-to-all-start.2 = ((bf16[8,160,128]{2,1,0:T(8,128)(2,1)}), bf16[8,160,128]{2,1,0:T(8,128)(2,1)S(1)}, u32[]{:S(2)}, u32[]{:S(2)}) async-start(bf16[8,160,128]{2,1,0:T(8,128)(2,1)} %get-tuple-element.35), calls=%async_computation.2 | async-start | bytes 655360 | tf_op jit(solution)/shard_map/all_to_all | solution.py:494
  84.0 2.1 %collective-permute-done.8.refs_4_ = bf16[80,4096]{1,0:T(8,128)(2,1)} collective-permute-done((bf16[80,4096]{1,0:T(8,128)(2,1)}, bf16[80,4096]{1,0:T(8,128)(2,1)}, u32[]{:S(2)}, u32[]{:S(2)}) %collective-permute-start.8) | collective-permute-done | bytes 655392 | tf_op jit(solution)/shard_map/ppermute | solution.py:476
  86.0 2.8 %collective-permute-start.9 = (bf16[80,4096]{1,0:T(8,128)(2,1)}, bf16[80,4096]{1,0:T(8,128)(2,1)S(1)}, u32[]{:S(2)}, u32[]{:S(2)}) collective-permute-start(bf16[80,4096]{1,0:T(8,128)(2,1)} %collective-permute-done.8.refs_4_), channel_id=1, source_target_pairs={{0,64},{8,456},{64,128},{72,8},{128,192},{136,72},{192,256},{200,1... | collective-permute-start | bytes 1966088 | tf_op jit(solution)/shard_map/ppermute | solution.py:476
  88.9 4.1 %collective-permute-done.6.refs_0_ = bf16[80,4096]{1,0:T(8,128)(2,1)S(1)} collective-permute-done((bf16[80,4096]{1,0:T(8,128)(2,1)}, bf16[80,4096]{1,0:T(8,128)(2,1)S(1)}, u32[]{:S(2)}, u32[]{:S(2)}) %collective-permute-start.6) | collective-permute-done | bytes 655392 | tf_op jit(solution)/shard_map/ppermute | solution.py:476
  92.9 2.8 %collective-permute-start.10 = (bf16[80,4096]{1,0:T(8,128)(2,1)S(1)}, bf16[80,4096]{1,0:T(8,128)(2,1)S(1)}, u32[]{:S(2)}, u32[]{:S(2)}) collective-permute-start(bf16[80,4096]{1,0:T(8,128)(2,1)S(1)} %collective-permute-done.6.refs_0_), channel_id=1, source_target_pairs={{0,64},{8,456},{64,128},{72,8},{128,192},{136,72},{192,256},{200,1... | collective-permute-start | bytes 1966088 | tf_op jit(solution)/shard_map/ppermute | solution.py:476
  95.8 0.0 all-to-all-done.2.refs_1_
  95.8 0.0 copy-done.1
  95.8 1.3 group.1
  97.1 0.0 copy-start.2
  97.1 0.6 copy-done.2
  97.7 3.4 %all-to-all-start.3 = ((bf16[8,160,128]{2,1,0:T(8,128)(2,1)}), bf16[8,160,128]{2,1,0:T(8,128)(2,1)S(1)}, u32[]{:S(2)}, u32[]{:S(2)}) async-start(bf16[8,160,128]{2,1,0:T(8,128)(2,1)} %get-tuple-element.40), calls=%async_computation.3 | async-start | bytes 655360 | tf_op jit(solution)/shard_map/all_to_all | solution.py:502
  101.1 0.6 pad_add_fusion.place_ref
  101.8 7.3 %expand_early.1 = (bf16[192,400]{1,0:T(8,128)(2,1)}, bf16[192,400]{1,0:T(8,128)(2,1)}) custom-call(bf16[80,4096]{1,0:T(8,128)(2,1)} %copy-done, bf16[80,4096]{1,0:T(8,128)(2,1)} %copy-done.8, bf16[80,4096]{1,0:T(8,128)(2,1)} %collective-permute-done.7.refs_2_, bf16[80,4096]{1,0:T(8,128)(2,1)} %collective-permute-done.5.refs_3_, ...), custom_call_target="tpu_custom_call" | custom-call | flops 2516582400 | bytes 8388608 | tf_op jit(solution)/shard_map/expand_early/pallas_call | solution.py:147
  109.1 0.0 copy-done.5
  109.1 0.0 copy-done.3
  109.1 5.0 %collective-permute-start.12 = (bf16[192,400]{1,0:T(8,128)(2,1)}, bf16[192,400]{1,0:T(8,128)(2,1)S(1)}, u32[]{:S(2)}, u32[]{:S(2)}) collective-permute-start(bf16[192,400]{1,0:T(8,128)(2,1)} %get-tuple-element.48), channel_id=1, source_target_pairs={{0,8},{8,0},{1,9},{9,1},{2,10},{10,2},{3,11},{11,3},{4,12},{12,4},... | collective-permute-start | bytes 460808 | tf_op jit(solution)/shard_map/ppermute | solution.py:515
  114.1 0.0 collective-permute-done.9.refs_1_
  114.1 0.0 copy-start.6
  114.1 0.0 collective-permute-done.10.refs_2_
  114.1 0.8 copy-done.6
  114.9 0.8 copy-done.7
  115.8 4.2 %expand_other.1 = bf16[192,240]{1,0:T(8,128)(2,1)} custom-call(bf16[80,4096]{1,0:T(8,128)(2,1)} %copy-done.5, bf16[80,4096]{1,0:T(8,128)(2,1)} %copy-done.6, bf16[80,4096]{1,0:T(8,128)(2,1)} %copy-done.7, bf16[192,4096]{1,0:T(8,128)(2,1)} %copy-done.4, bf16[192,4096]{1,0:T(8,128)(2,1)} %collective-permute-done.2.refs_4_.refs_6_), custom_call_target="tpu_custom_call" | custom-call | flops 754974720 | bytes 8388608 | tf_op jit(solution)/shard_map/expand_other/pallas_call | solution.py:147
  120.0 1.9 %collective-permute-start.11 = (bf16[192,240]{1,0:T(8,128)(2,1)}, bf16[192,240]{1,0:T(8,128)(2,1)S(1)}, u32[]{:S(2)}, u32[]{:S(2)}) collective-permute-start(bf16[192,240]{1,0:T(8,128)(2,1)} %expand_other.1), channel_id=1, source_target_pairs={{0,8},{8,0},{1,9},{9,1},{2,10},{10,2},{3,11},{11,3},{4,12},{12,4},... | collective-permute-start | bytes 276488 | tf_op jit(solution)/shard_map/ppermute | solution.py:515
  121.9 0.0 all-to-all-done.3.refs_2_
  121.9 0.0 copy-start.9
  121.9 0.7 copy-done.9
  122.6 5.7 %finish.1 = bf16[128,1024]{1,0:T(8,128)(2,1)} custom-call(s32[1]{0:T(128)} %bitcast.5.refs_0_, f32[32,128]{1,0:T(8,128)} %reduce_sum.9.refs_0_.refs_1_, bf16[8,160,128]{2,1,0:T(8,128)(2,1)} %copy-done.9, f32[128,128]{1,0:T(8,128)} %get-tuple-element.34.refs_3_.refs_2_, f32[128,128]{1,0:T(8,128)} %copy-done.2, f32[8,128]{1,0:T(8,128)} %copy-done.3, ...), custom_call_target="tpu_custom_call" | custom-call | flops 2147483648 | bytes 4194304 | tf_op jit(solution)/shard_map/finish/pallas_call | solution.py:55
  128.3 0.0 collective-permute-done.11.refs_7_
  128.3 0.0 copy-start.11
  128.3 0.0 collective-permute-done.12.refs_6_
  128.4 0.6 copy-done.11
  129.0 0.1 copy-done.10
  129.0 7.3 %last.1 = bf16[192,1280]{1,0:T(8,128)(2,1)} custom-call(s32[2]{0:T(128)} %pad_add_fusion.place_ref, bf16[80,4096]{1,0:T(8,128)(2,1)} %copy-done.5, bf16[80,4096]{1,0:T(8,128)(2,1)} %copy-done.6, bf16[80,4096]{1,0:T(8,128)(2,1)} %copy-done.7, bf16[192,4096]{1,0:T(8,128)(2,1)} %bitcast.12, bf16[192,4096]{1,0:T(8,128)(2,1)} %bitcast.15, ...), custom_call_target="tpu_custom_call" | custom-call | flops 1073741824 | bytes 8388608 | tf_op jit(solution)/shard_map/last/pallas_call | solution.py:223
  (8 shorter events, 0.0 us)
Async XLA Ops:
  0.6 35.8 %collective-permute-start.1 = (bf16[192,4096]{1,0:T(8,128)(2,1)}, bf16[192,4096]{1,0:T(8,128)(2,1)S(1)}, u32[]{:S(2)}, u32[]{:S(2)}) collective-permute-start(bf16[192,4096]{1,0:T(8,128)(2,1)} %bitcast.10), channel_id=1, source_target_pairs={{0,8},{8,0},{1,9},{9,1},{2,10},{10,2},{3,11},{11,3},{4,12},{12,4},... | collective-permute-start | bytes 4718600 | tf_op jit(solution)/shard_map/ppermute | solution.py:461
  9.4 27.0 %collective-permute-start.2 = (bf16[192,4096]{1,0:T(8,128)(2,1)}, bf16[192,4096]{1,0:T(8,128)(2,1)}, u32[]{:S(2)}, u32[]{:S(2)}) collective-permute-start(bf16[192,4096]{1,0:T(8,128)(2,1)} %bitcast.13), channel_id=1, source_target_pairs={{0,8},{8,0},{1,9},{9,1},{2,10},{10,2},{3,11},{11,3},{4,12},{12,4},... | collective-permute-start | bytes 4718600 | tf_op jit(solution)/shard_map/ppermute | solution.py:461
  13.5 23.0 %all-to-all-start = ((bf16[32,40,256]{2,1,0:T(8,128)(2,1)}), bf16[32,40,256]{2,1,0:T(8,128)(2,1)S(1)}, u32[]{:S(2)}, u32[]{:S(2)}) async-start(bf16[32,40,256]{2,1,0:T(8,128)(2,1)} %place.1), calls=%async_computation | async-start | bytes 1310720 | tf_op jit(solution)/shard_map/all_to_all | solution.py:430
  18.5 4.8 %collective-permute-start = (bf16[3,1024]{1,0:T(4,128)(2,1)S(1)}, bf16[3,1024]{1,0:T(4,128)(2,1)S(1)}, u32[]{:S(2)}, u32[]{:S(2)}) collective-permute-start(bf16[3,1024]{1,0:T(4,128)(2,1)S(1)} %slice.3), channel_id=1, source_target_pairs={{0,8},{8,16},{16,24},{24,32},{32,40},{40,48},{48,56},{56,64},{64,7... | collective-permute-start | bytes 18440 | tf_op jit(solution)/shard_map/ppermute | solution.py:419
  23.4 0.6 copy-start.12
  36.5 37.6 %copy-start.4 = (bf16[192,4096]{1,0:T(8,128)(2,1)}, bf16[192,4096]{1,0:T(8,128)(2,1)S(1)}, u32[]{:S(2)}) copy-start(bf16[192,4096]{1,0:T(8,128)(2,1)S(1)} %collective-permute-done.1.refs_3_.refs_5_) | copy-start | bytes 4718596
  37.1 37.0 %copy-start = (bf16[80,4096]{1,0:T(8,128)(2,1)}, bf16[80,4096]{1,0:T(8,128)(2,1)S(1)}, u32[]{:S(2)}) copy-start(bf16[80,4096]{1,0:T(8,128)(2,1)S(1)} %assemble.1.refs_0_) | copy-start | bytes 1966084
  37.1 15.2 %collective-permute-start.4 = (bf16[80,4096]{1,0:T(8,128)(2,1)S(1)}, bf16[80,4096]{1,0:T(8,128)(2,1)}, u32[]{:S(2)}, u32[]{:S(2)}) collective-permute-start(bf16[80,4096]{1,0:T(8,128)(2,1)S(1)} %assemble.1.refs_0_), channel_id=1, source_target_pairs={{0,8},{8,0},{1,9},{9,1},{2,10},{10,2},{3,11},{11,3},{4,12},{12,4},... | collective-permute-start | bytes 1966088 | tf_op jit(solution)/shard_map/ppermute | solution.py:478
  41.6 18.2 %collective-permute-start.3 = (bf16[80,4096]{1,0:T(8,128)(2,1)S(1)}, bf16[80,4096]{1,0:T(8,128)(2,1)S(1)}, u32[]{:S(2)}, u32[]{:S(2)}) collective-permute-start(bf16[80,4096]{1,0:T(8,128)(2,1)S(1)} %assemble.1.refs_0_), channel_id=1, source_target_pairs={{0,64},{8,456},{64,128},{72,8},{128,192},{136,72},{192,256},{200,1... | collective-permute-start | bytes 1966088 | tf_op jit(solution)/shard_map/ppermute | solution.py:476
  52.3 11.2 %all-to-all-start.1 = ((f32[8,32,128]{2,1,0:T(8,128)}), f32[8,32,128]{2,1,0:T(8,128)S(1)}, u32[]{:S(2)}, u32[]{:S(2)}) async-start(f32[8,32,128]{2,1,0:T(8,128)} %get-tuple-element.29), calls=%async_computation.1 | async-start | bytes 262144 | tf_op jit(solution)/shard_map/all_to_all | solution.py:481
  55.7 18.4 %collective-permute-start.7 = (bf16[80,4096]{1,0:T(8,128)(2,1)}, bf16[80,4096]{1,0:T(8,128)(2,1)}, u32[]{:S(2)}, u32[]{:S(2)}) collective-permute-start(bf16[80,4096]{1,0:T(8,128)(2,1)} %collective-permute-done.4), channel_id=1, source_target_pairs={{0,64},{8,456},{64,128},{72,8},{128,192},{136,72},{192,256},{200,1... | collective-permute-start | bytes 1966088 | tf_op jit(solution)/shard_map/ppermute | solution.py:476
  59.8 14.3 %copy-start.8 = (bf16[80,4096]{1,0:T(8,128)(2,1)}, bf16[80,4096]{1,0:T(8,128)(2,1)S(1)}, u32[]{:S(2)}) copy-start(bf16[80,4096]{1,0:T(8,128)(2,1)S(1)} %collective-permute-done.3.refs_1_) | copy-start | bytes 1966084
  63.5 12.5 %collective-permute-start.5 = (bf16[80,4096]{1,0:T(8,128)(2,1)S(1)}, bf16[80,4096]{1,0:T(8,128)(2,1)}, u32[]{:S(2)}, u32[]{:S(2)}) collective-permute-start(bf16[80,4096]{1,0:T(8,128)(2,1)S(1)} %collective-permute-done.3.refs_1_), channel_id=1, source_target_pairs={{0,64},{8,456},{64,128},{72,8},{128,192},{136,72},{192,256},{200,1... | collective-permute-start | bytes 1966088 | tf_op jit(solution)/shard_map/ppermute | solution.py:476
  67.0 28.8 %copy-start.1 = (f32[128,128]{1,0:T(8,128)S(1)}, f32[128,128]{1,0:T(8,128)}, u32[]{:S(2)}) copy-start(f32[128,128]{1,0:T(8,128)} %get-tuple-element.34.refs_3_.refs_2_) | copy-start | bytes 196612
  74.1 11.9 %collective-permute-start.8 = (bf16[80,4096]{1,0:T(8,128)(2,1)}, bf16[80,4096]{1,0:T(8,128)(2,1)}, u32[]{:S(2)}, u32[]{:S(2)}) collective-permute-start(bf16[80,4096]{1,0:T(8,128)(2,1)} %collective-permute-done.7.refs_2_), channel_id=1, source_target_pairs={{0,64},{8,456},{64,128},{72,8},{128,192},{136,72},{192,256},{200,1... | collective-permute-start | bytes 1966088 | tf_op jit(solution)/shard_map/ppermute | solution.py:476
  76.0 16.9 %collective-permute-start.6 = (bf16[80,4096]{1,0:T(8,128)(2,1)}, bf16[80,4096]{1,0:T(8,128)(2,1)S(1)}, u32[]{:S(2)}, u32[]{:S(2)}) collective-permute-start(bf16[80,4096]{1,0:T(8,128)(2,1)} %collective-permute-done.5.refs_3_), channel_id=1, source_target_pairs={{0,64},{8,456},{64,128},{72,8},{128,192},{136,72},{192,256},{200,1... | collective-permute-start | bytes 1966088 | tf_op jit(solution)/shard_map/ppermute | solution.py:476
  79.1 16.7 %all-to-all-start.2 = ((bf16[8,160,128]{2,1,0:T(8,128)(2,1)}), bf16[8,160,128]{2,1,0:T(8,128)(2,1)S(1)}, u32[]{:S(2)}, u32[]{:S(2)}) async-start(bf16[8,160,128]{2,1,0:T(8,128)(2,1)} %get-tuple-element.35), calls=%async_computation.2 | async-start | bytes 655360 | tf_op jit(solution)/shard_map/all_to_all | solution.py:494
  86.0 28.1 %collective-permute-start.9 = (bf16[80,4096]{1,0:T(8,128)(2,1)}, bf16[80,4096]{1,0:T(8,128)(2,1)S(1)}, u32[]{:S(2)}, u32[]{:S(2)}) collective-permute-start(bf16[80,4096]{1,0:T(8,128)(2,1)} %collective-permute-done.8.refs_4_), channel_id=1, source_target_pairs={{0,64},{8,456},{64,128},{72,8},{128,192},{136,72},{192,256},{200,1... | collective-permute-start | bytes 1966088 | tf_op jit(solution)/shard_map/ppermute | solution.py:476
  92.9 16.1 %copy-start.5 = (bf16[80,4096]{1,0:T(8,128)(2,1)}, bf16[80,4096]{1,0:T(8,128)(2,1)S(1)}, u32[]{:S(2)}) copy-start(bf16[80,4096]{1,0:T(8,128)(2,1)S(1)} %collective-permute-done.6.refs_0_) | copy-start | bytes 1966084
  92.9 21.2 %collective-permute-start.10 = (bf16[80,4096]{1,0:T(8,128)(2,1)S(1)}, bf16[80,4096]{1,0:T(8,128)(2,1)S(1)}, u32[]{:S(2)}, u32[]{:S(2)}) collective-permute-start(bf16[80,4096]{1,0:T(8,128)(2,1)S(1)} %collective-permute-done.6.refs_0_), channel_id=1, source_target_pairs={{0,64},{8,456},{64,128},{72,8},{128,192},{136,72},{192,256},{200,1... | collective-permute-start | bytes 1966088 | tf_op jit(solution)/shard_map/ppermute | solution.py:476
  97.1 0.6 copy-start.2
  97.7 11.4 %copy-start.3 = (f32[8,128]{1,0:T(8,128)}, f32[8,128]{1,0:T(8,128)S(1)}, u32[]{:S(2)}) copy-start(f32[8,128]{1,0:T(8,128)S(1)} %get-tuple-element.42.refs_5_) | copy-start | bytes 12292
  97.7 24.2 %all-to-all-start.3 = ((bf16[8,160,128]{2,1,0:T(8,128)(2,1)}), bf16[8,160,128]{2,1,0:T(8,128)(2,1)S(1)}, u32[]{:S(2)}, u32[]{:S(2)}) async-start(bf16[8,160,128]{2,1,0:T(8,128)(2,1)} %get-tuple-element.40), calls=%async_computation.3 | async-start | bytes 655360 | tf_op jit(solution)/shard_map/all_to_all | solution.py:502
  109.1 19.2 %collective-permute-start.12 = (bf16[192,400]{1,0:T(8,128)(2,1)}, bf16[192,400]{1,0:T(8,128)(2,1)S(1)}, u32[]{:S(2)}, u32[]{:S(2)}) collective-permute-start(bf16[192,400]{1,0:T(8,128)(2,1)} %get-tuple-element.48), channel_id=1, source_target_pairs={{0,8},{8,0},{1,9},{9,1},{2,10},{10,2},{3,11},{11,3},{4,12},{12,4},... | collective-permute-start | bytes 460808 | tf_op jit(solution)/shard_map/ppermute | solution.py:515
  114.1 0.8 copy-start.6
  114.9 0.9 copy-start.7
  120.0 8.3 %collective-permute-start.11 = (bf16[192,240]{1,0:T(8,128)(2,1)}, bf16[192,240]{1,0:T(8,128)(2,1)S(1)}, u32[]{:S(2)}, u32[]{:S(2)}) collective-permute-start(bf16[192,240]{1,0:T(8,128)(2,1)} %expand_other.1), channel_id=1, source_target_pairs={{0,8},{8,0},{1,9},{9,1},{2,10},{10,2},{3,11},{11,3},{4,12},{12,4},... | collective-permute-start | bytes 276488 | tf_op jit(solution)/shard_map/ppermute | solution.py:515
  121.9 0.7 copy-start.9
  128.3 0.6 copy-start.11
  128.3 0.7 copy-start.10

commit v2 on v1

--- a/solution.py
+++ b/solution.py
@@ -19,7 +19,7 @@
 WHOLE = pl.BlockSpec(memory_space=pltpu.HBM)
 
 
-def call(kernel, out_shape, in_specs, scratch=(), name=None, vmem=60, flops=0):
+def call(kernel, out_shape, in_specs, scratch=(), name=None, vmem=60, flops=0, lazy=False):
     single = not isinstance(out_shape, tuple)
     outs = (out_shape,) if single else out_shape
 
@@ -39,10 +39,13 @@
                 inputs[index] = held[place]
             for copy in copies:
                 copy.start()
-            for copy in copies:
-                copy.wait()
             made = held[len(moved) :]
-            kernel(*inputs, *made, *rest)
+            if lazy:
+                kernel(copies, *inputs, *made, *rest)
+            else:
+                for copy in copies:
+                    copy.wait()
+                kernel(*inputs, *made, *rest)
             copies = [
                 pltpu.make_async_copy(source, target, sems.at[len(moved) + place])
                 for place, (source, target) in enumerate(zip(made, results))
@@ -182,16 +185,10 @@
         pltpu.make_async_copy(source, target, sems.at[index])
         for index, (source, target) in enumerate(zip(sources, targets))
     ]
-    for copy in copies:
+    for copy in copies[5:] + copies[:5]:
         copy.start()
-    for copy in copies:
-        copy.wait()
-    both = lax.dot_general(
-        weight[...], rows[...], (((1,), (1,)), ((), ())), preferred_element_type=F32
-    )
-    mine_late[...] = (silu(both[:units]) * both[units:]).astype(BF16)
-    places = []
-    for pair, blocks in (((mine_early, other_early), EARLY), ((mine_late, other_late), LATE)):
+
+    def ordered(pair, blocks, first):
         count = pair[0].shape[1]
         row = lax.broadcasted_iota(jnp.int32, (count, 1), 0)
         block = divided(row, 4 * CAP)
@@ -201,17 +198,30 @@
             steps = jnp.where(block == index, step, steps)
             twin = jnp.where(block == index, other, twin)
         base = within + divided(within, CAP) * CAP
+        places = []
         for ref, holder in zip(pair, (place_ref[1], 1 - place_ref[1])):
             layer = (place_ref[0] + steps * (2 * holder - 1)) & 7
             core = holder + twin * (1 - 2 * holder)
             places.append((ref, layer * (8 * CAP) + core * CAP + base))
-    for start in range(0, out.shape[1], 256):
-        total = jnp.zeros((units, 256), F32)
-        for ref, target in places:
-            column = lax.broadcasted_iota(jnp.int32, (ref.shape[1], 256), 1) + start
-            table = jnp.where(column == target, 1.0, 0.0).astype(BF16)
-            total = total + jnp.dot(ref[...], table, preferred_element_type=F32)
-        out[:, start : start + 256] = total.astype(BF16)
+        for start in range(0, out.shape[1], 256):
+            here = slice(start, start + 256)
+            total = jnp.zeros((units, 256), F32) if first else out[:, here].astype(F32)
+            for ref, target in places:
+                column = lax.broadcasted_iota(jnp.int32, (count, 256), 1) + start
+                table = jnp.where(column == target, 1.0, 0.0).astype(BF16)
+                total = total + jnp.dot(ref[...], table, preferred_element_type=F32)
+            out[:, here] = total.astype(BF16)
+
+    for copy in copies[5:7]:
+        copy.wait()
+    ordered((mine_early, other_early), EARLY, True)
+    for copy in copies[7:] + copies[:5]:
+        copy.wait()
+    both = lax.dot_general(
+        weight[...], rows[...], (((1,), (1,)), ((), ())), preferred_element_type=F32
+    )
+    mine_late[...] = (silu(both[:units]) * both[units:]).astype(BF16)
+    ordered((mine_late, other_late), LATE, False)
     copy = pltpu.make_async_copy(out, out_ref, sems.at[0])
     copy.start()
     copy.wait()
@@ -358,6 +368,7 @@
 
 
 def finish_kernel(
+    copies,
     mine_ref,
     coef_ref,
     got_ref,
@@ -373,6 +384,8 @@
     dense,
 ):
     rows, width = conv_ref.shape
+    for copy in copies[:4]:
+        copy.wait()
     rates = [rate_ref[n * 8 : n * 8 + 8, :] for n in range(16)]
     zero = jnp.zeros((8, 128), F32)
     states, _ = fold(got_ref, rates, mine_ref[0], [zero] * 16, zero)
@@ -380,6 +393,9 @@
         jnp.exp2(rates[n] * before_step_ref[...]) * states[n] + before_ref[n * 8 : n * 8 + 8, :]
         for n in range(16)
     ]
+
+    for copy in copies[4:6]:
+        copy.wait()
 
     def advance(token, carry):
         here = pl.ds(pl.multiple_of(token * 8, 8), 8)
@@ -393,6 +409,8 @@
         return carry
 
     lax.fori_loop(0, rows, advance, 0, unroll=4)
+    for copy in copies[6:]:
+        copy.wait()
     for index in range(width // 128):
         lanes = slice(index * 128, index * 128 + 128)
         value = dense[pl.ds(index, rows, stride=8), :]
@@ -506,7 +524,7 @@
         shape((rows, width), BF16),
         [SMEM, SMEM] + [WHOLE] * 9,
         [pltpu.VMEM(dense.shape, F32)],
-        name="finish", flops=1 << 31,
+        lazy=True, name="finish", flops=1 << 31,
     )(layer, coef, far, rate, before, before_step, local, sums, conv, skip_gain[None], inner_z)
 
     other_early, mine_early = expand([block, own[1], twin[1], own[2], twin[2]], pairs, "expand_early")

time: 138 us -> 136 us (0.986)
  Pallas kernels: 39.2 us -> 37.8 us
where the time goes in v2:
time: 136 us; the launch traced here: 135 us
  starting transfers between devices  68.6 us (50%)
  Pallas kernels  37.8 us (28%)
  waiting for transfers between devices  21.3 us (16%)
  local copies, waits for them, and re-layouts  5.04 us (4%)
    ppermute x7, starting transfers between devices, step_on(): return lax.ppermute(rows, ('z', 'c'), onward)  26.3 us
    pallas_call x6, Pallas kernels, run(): pl.pallas_call(body, out_shape=outs, in_specs=in_specs, out_specs=(WHOLE,...  20.1 us
    pallas_call x2, Pallas kernels, expand(): pl.pallas_call(functools.partial(expand_kernel, len(blocks), total), out_...  11.5 us
    ppermute x2, starting transfers between devices, shards(): others = [lax.ppermute(weight, 'c', swap) for weight in weights]  10.7 us
    all_to_all x1, waiting for transfers between devices, shards(): lax.all_to_all(placed, ('exp', 'x'), split_axis=0, concat_axis=0, tiled=T...  8.68 us
    ppermute x7, waiting for transfers between devices, step_on(): return lax.ppermute(rows, ('z', 'c'), onward)  8.08 us
    ppermute x2, starting transfers between devices, shards(): lax.ppermute(part, 'c', swap)  6.89 us
    pallas_call x1, Pallas kernels, last(): pl.pallas_call(last_kernel, out_shape=out, in_specs=[SMEM] + [WHOLE] * 8,...  6.25 us
  transfers between devices with their start and end apart: 17, of which 6 were waited for; matrix products, arithmetic and copies ran while one was open for 1% of the time, Pallas kernels for 23%

profile of v2, /device:TPU:1, one launch (start us, length us, event | category | flops | bytes accessed | tf_op | source)
XLA Modules:
  0.0 135.0 jit_solution(2597644942293216558)
XLA Ops:
  0.6 8.8 %collective-permute-start.1 = (bf16[192,4096]{1,0:T(8,128)(2,1)}, bf16[192,4096]{1,0:T(8,128)(2,1)S(1)}, u32[]{:S(2)}, u32[]{:S(2)}) collective-permute-start(bf16[192,4096]{1,0:T(8,128)(2,1)} %bitcast.10), channel_id=1, source_target_pairs={{0,8},{8,0},{1,9},{9,1},{2,10},{10,2},{3,11},{11,3},{4,12},{12,4},... | collective-permute-start | bytes 4718600 | tf_op jit(solution)/shard_map/ppermute | solution.py:479
  9.4 1.9 %collective-permute-start.2 = (bf16[192,4096]{1,0:T(8,128)(2,1)}, bf16[192,4096]{1,0:T(8,128)(2,1)}, u32[]{:S(2)}, u32[]{:S(2)}) collective-permute-start(bf16[192,4096]{1,0:T(8,128)(2,1)} %bitcast.13), channel_id=1, source_target_pairs={{0,8},{8,0},{1,9},{9,1},{2,10},{10,2},{3,11},{11,3},{4,12},{12,4},... | collective-permute-start | bytes 4718600 | tf_op jit(solution)/shard_map/ppermute | solution.py:479
  11.4 2.1 %place.1 = bf16[32,40,256]{2,1,0:T(8,128)(2,1)} custom-call(s32[2,128]{1,0:T(2,128)} %bitcast.20, bf16[128,512]{1,0:T(8,128)(2,1)} %refs_1_.1), custom_call_target="tpu_custom_call" | custom-call | flops 268435456 | bytes 4194304 | tf_op jit(solution)/shard_map/place/pallas_call | solution.py:58
  13.5 4.3 %all-to-all-start = ((bf16[32,40,256]{2,1,0:T(8,128)(2,1)}), bf16[32,40,256]{2,1,0:T(8,128)(2,1)S(1)}, u32[]{:S(2)}, u32[]{:S(2)}) async-start(bf16[32,40,256]{2,1,0:T(8,128)(2,1)} %place.1), calls=%async_computation | async-start | bytes 1310720 | tf_op jit(solution)/shard_map/all_to_all | solution.py:448
  17.8 0.7 slice.3
  18.5 4.1 %collective-permute-start = (bf16[3,1024]{1,0:T(4,128)(2,1)S(1)}, bf16[3,1024]{1,0:T(4,128)(2,1)S(1)}, u32[]{:S(2)}, u32[]{:S(2)}) collective-permute-start(bf16[3,1024]{1,0:T(4,128)(2,1)S(1)} %slice.3), channel_id=1, source_target_pairs={{0,8},{8,16},{16,24},{24,32},{32,40},{40,48},{48,56},{56,64},{64,7... | collective-permute-start | bytes 18440 | tf_op jit(solution)/shard_map/ppermute | solution.py:437
  22.6 0.8 collective-permute-done.refs_1_
  23.4 0.6 copy-done.12
  24.0 3.8 %conv.1 = (f32[128,1024]{1,0:T(8,128)}, f32[1024,128]{1,0:T(8,128)}, f32[1024,128]{1,0:T(8,128)}, f32[128,128]{1,0:T(8,128)}, f32[8,32,128]{2,1,0:T(8,128)}) custom-call(bf16[128,1024]{1,0:T(8,128)(2,1)} %refs_0_.1, bf16[3,1024]{1,0:T(4,128)(2,1)} %copy-done.12, bf16[128,1024]{1,0:T(8,128)(2,1)} %refs_2_.1, f32[4,1024]{1,0:T(4,128)} %refs_3_.1, ...), custom_call_target="tpu_custom_call" | custom-call | flops 536870912 | bytes 4194304 | tf_op jit(solution)/shard_map/conv/pallas_call | solution.py:58
  27.8 8.7 %all-to-all-done.refs_0_ = bf16[32,40,256]{2,1,0:T(8,128)(2,1)S(1)} async-done(((bf16[32,40,256]{2,1,0:T(8,128)(2,1)}), bf16[32,40,256]{2,1,0:T(8,128)(2,1)S(1)}, u32[]{:S(2)}, u32[]{:S(2)}) %all-to-all-start) | async-done | bytes 655392 | tf_op jit(solution)/shard_map/all_to_all | solution.py:448
  36.5 0.0 collective-permute-done.1.refs_3_.refs_5_
  36.5 0.0 collective-permute-done.2.refs_4_.refs_6_
  36.5 0.6 assemble.1.refs_0_
  37.1 0.0 copy-start
  37.1 4.5 %collective-permute-start.4 = (bf16[80,4096]{1,0:T(8,128)(2,1)S(1)}, bf16[80,4096]{1,0:T(8,128)(2,1)}, u32[]{:S(2)}, u32[]{:S(2)}) collective-permute-start(bf16[80,4096]{1,0:T(8,128)(2,1)S(1)} %assemble.1.refs_0_), channel_id=1, source_target_pairs={{0,8},{8,0},{1,9},{9,1},{2,10},{10,2},{3,11},{11,3},{4,12},{12,4},... | collective-permute-start | bytes 1966088 | tf_op jit(solution)/shard_map/ppermute | solution.py:496
  41.6 10.7 %collective-permute-start.3 = (bf16[80,4096]{1,0:T(8,128)(2,1)S(1)}, bf16[80,4096]{1,0:T(8,128)(2,1)S(1)}, u32[]{:S(2)}, u32[]{:S(2)}) collective-permute-start(bf16[80,4096]{1,0:T(8,128)(2,1)S(1)} %assemble.1.refs_0_), channel_id=1, source_target_pairs={{0,64},{8,456},{64,128},{72,8},{128,192},{136,72},{192,256},{200,1... | collective-permute-start | bytes 1966088 | tf_op jit(solution)/shard_map/ppermute | solution.py:494
  52.3 0.0 collective-permute-done.4
  52.3 3.4 %all-to-all-start.1 = ((f32[8,32,128]{2,1,0:T(8,128)}), f32[8,32,128]{2,1,0:T(8,128)S(1)}, u32[]{:S(2)}, u32[]{:S(2)}) async-start(f32[8,32,128]{2,1,0:T(8,128)} %get-tuple-element.29), calls=%async_computation.1 | async-start | bytes 262144 | tf_op jit(solution)/shard_map/all_to_all | solution.py:499
  55.7 2.2 %collective-permute-start.7 = (bf16[80,4096]{1,0:T(8,128)(2,1)}, bf16[80,4096]{1,0:T(8,128)(2,1)}, u32[]{:S(2)}, u32[]{:S(2)}) collective-permute-start(bf16[80,4096]{1,0:T(8,128)(2,1)} %collective-permute-done.4), channel_id=1, source_target_pairs={{0,64},{8,456},{64,128},{72,8},{128,192},{136,72},{192,256},{200,1... | collective-permute-start | bytes 1966088 | tf_op jit(solution)/shard_map/ppermute | solution.py:494
  57.9 1.9 %collective-permute-done.3.refs_1_ = bf16[80,4096]{1,0:T(8,128)(2,1)S(1)} collective-permute-done((bf16[80,4096]{1,0:T(8,128)(2,1)S(1)}, bf16[80,4096]{1,0:T(8,128)(2,1)S(1)}, u32[]{:S(2)}, u32[]{:S(2)}) %collective-permute-start.3) | collective-permute-done | bytes 655392 | tf_op jit(solution)/shard_map/ppermute | solution.py:494
  59.8 3.7 %all-to-all-done.1 = f32[8,32,128]{2,1,0:T(8,128)S(1)} async-done(((f32[8,32,128]{2,1,0:T(8,128)}), f32[8,32,128]{2,1,0:T(8,128)S(1)}, u32[]{:S(2)}, u32[]{:S(2)}) %all-to-all-start.1) | async-done | bytes 131104 | tf_op jit(solution)/shard_map/all_to_all | solution.py:499
  63.5 2.9 %collective-permute-start.5 = (bf16[80,4096]{1,0:T(8,128)(2,1)S(1)}, bf16[80,4096]{1,0:T(8,128)(2,1)}, u32[]{:S(2)}, u32[]{:S(2)}) collective-permute-start(bf16[80,4096]{1,0:T(8,128)(2,1)S(1)} %collective-permute-done.3.refs_1_), channel_id=1, source_target_pairs={{0,64},{8,456},{64,128},{72,8},{128,192},{136,72},{192,256},{200,1... | collective-permute-start | bytes 1966088 | tf_op jit(solution)/shard_map/ppermute | solution.py:494
  66.4 0.6 reduce_sum.9.refs_0_.refs_1_
  67.0 7.0 %scan.1 = (f32[1024,128]{1,0:T(8,128)}, f32[1024,128]{1,0:T(8,128)}, bf16[8,160,128]{2,1,0:T(8,128)(2,1)}) custom-call(f32[32,128]{1,0:T(8,128)} %reduce_sum.9.refs_0_.refs_1_, f32[1024,128]{1,0:T(8,128)} %get-tuple-element.32.refs_1_, f32[1024,128]{1,0:T(8,128)} %get-tuple-element.33.refs_2_, f32[128,128]{1,0:T(8,128)} %get-tuple-element.34.refs_3_.refs_2_), custom_call_target="tpu_custom_call" | custom-call | flops 2147483648 | bytes 4194304 | tf_op jit(solution)/shard_map/scan/pallas_call | solution.py:58
  74.0 0.0 copy-done.4
  74.1 0.0 copy-done
  74.1 0.0 copy-done.8
  74.1 0.0 collective-permute-done.7.refs_2_
  74.1 1.9 %collective-permute-start.8 = (bf16[80,4096]{1,0:T(8,128)(2,1)}, bf16[80,4096]{1,0:T(8,128)(2,1)}, u32[]{:S(2)}, u32[]{:S(2)}) collective-permute-start(bf16[80,4096]{1,0:T(8,128)(2,1)} %collective-permute-done.7.refs_2_), channel_id=1, source_target_pairs={{0,64},{8,456},{64,128},{72,8},{128,192},{136,72},{192,256},{200,1... | collective-permute-start | bytes 1966088 | tf_op jit(solution)/shard_map/ppermute | solution.py:494
  76.0 0.0 collective-permute-done.5.refs_3_
  76.0 3.0 %collective-permute-start.6 = (bf16[80,4096]{1,0:T(8,128)(2,1)}, bf16[80,4096]{1,0:T(8,128)(2,1)S(1)}, u32[]{:S(2)}, u32[]{:S(2)}) collective-permute-start(bf16[80,4096]{1,0:T(8,128)(2,1)} %collective-permute-done.5.refs_3_), channel_id=1, source_target_pairs={{0,64},{8,456},{64,128},{72,8},{128,192},{136,72},{192,256},{200,1... | collective-permute-start | bytes 1966088 | tf_op jit(solution)/shard_map/ppermute | solution.py:494
  79.1 4.9 %all-to-all-start.2 = ((bf16[8,160,128]{2,1,0:T(8,128)(2,1)}), bf16[8,160,128]{2,1,0:T(8,128)(2,1)S(1)}, u32[]{:S(2)}, u32[]{:S(2)}) async-start(bf16[8,160,128]{2,1,0:T(8,128)(2,1)} %get-tuple-element.35), calls=%async_computation.2 | async-start | bytes 655360 | tf_op jit(solution)/shard_map/all_to_all | solution.py:512
  84.0 2.1 %collective-permute-done.8.refs_4_ = bf16[80,4096]{1,0:T(8,128)(2,1)} collective-permute-done((bf16[80,4096]{1,0:T(8,128)(2,1)}, bf16[80,4096]{1,0:T(8,128)(2,1)}, u32[]{:S(2)}, u32[]{:S(2)}) %collective-permute-start.8) | collective-permute-done | bytes 655392 | tf_op jit(solution)/shard_map/ppermute | solution.py:494
  86.0 2.8 %collective-permute-start.9 = (bf16[80,4096]{1,0:T(8,128)(2,1)}, bf16[80,4096]{1,0:T(8,128)(2,1)S(1)}, u32[]{:S(2)}, u32[]{:S(2)}) collective-permute-start(bf16[80,4096]{1,0:T(8,128)(2,1)} %collective-permute-done.8.refs_4_), channel_id=1, source_target_pairs={{0,64},{8,456},{64,128},{72,8},{128,192},{136,72},{192,256},{200,1... | collective-permute-start | bytes 1966088 | tf_op jit(solution)/shard_map/ppermute | solution.py:494
  88.9 4.1 %collective-permute-done.6.refs_0_ = bf16[80,4096]{1,0:T(8,128)(2,1)S(1)} collective-permute-done((bf16[80,4096]{1,0:T(8,128)(2,1)}, bf16[80,4096]{1,0:T(8,128)(2,1)S(1)}, u32[]{:S(2)}, u32[]{:S(2)}) %collective-permute-start.6) | collective-permute-done | bytes 655392 | tf_op jit(solution)/shard_map/ppermute | solution.py:494
  92.9 2.8 %collective-permute-start.10 = (bf16[80,4096]{1,0:T(8,128)(2,1)S(1)}, bf16[80,4096]{1,0:T(8,128)(2,1)S(1)}, u32[]{:S(2)}, u32[]{:S(2)}) collective-permute-start(bf16[80,4096]{1,0:T(8,128)(2,1)S(1)} %collective-permute-done.6.refs_0_), channel_id=1, source_target_pairs={{0,64},{8,456},{64,128},{72,8},{128,192},{136,72},{192,256},{200,1... | collective-permute-start | bytes 1966088 | tf_op jit(solution)/shard_map/ppermute | solution.py:494
  95.8 0.0 all-to-all-done.2.refs_1_
  95.8 0.0 copy-done.1
  95.8 1.3 group.1
  97.1 0.0 copy-start.2
  97.1 0.6 copy-done.2
  97.7 3.4 %all-to-all-start.3 = ((bf16[8,160,128]{2,1,0:T(8,128)(2,1)}), bf16[8,160,128]{2,1,0:T(8,128)(2,1)S(1)}, u32[]{:S(2)}, u32[]{:S(2)}) async-start(bf16[8,160,128]{2,1,0:T(8,128)(2,1)} %get-tuple-element.40), calls=%async_computation.3 | async-start | bytes 655360 | tf_op jit(solution)/shard_map/all_to_all | solution.py:520
  101.1 0.6 pad_add_fusion.place_ref
  101.8 7.3 %expand_early.1 = (bf16[192,400]{1,0:T(8,128)(2,1)}, bf16[192,400]{1,0:T(8,128)(2,1)}) custom-call(bf16[80,4096]{1,0:T(8,128)(2,1)} %copy-done, bf16[80,4096]{1,0:T(8,128)(2,1)} %copy-done.8, bf16[80,4096]{1,0:T(8,128)(2,1)} %collective-permute-done.7.refs_2_, bf16[80,4096]{1,0:T(8,128)(2,1)} %collective-permute-done.5.refs_3_, ...), custom_call_target="tpu_custom_call" | custom-call | flops 2516582400 | bytes 8388608 | tf_op jit(solution)/shard_map/expand_early/pallas_call | solution.py:150
  109.1 0.0 copy-done.5
  109.1 0.0 copy-done.3
  109.1 5.0 %collective-permute-start.12 = (bf16[192,400]{1,0:T(8,128)(2,1)}, bf16[192,400]{1,0:T(8,128)(2,1)S(1)}, u32[]{:S(2)}, u32[]{:S(2)}) collective-permute-start(bf16[192,400]{1,0:T(8,128)(2,1)} %get-tuple-element.48), channel_id=1, source_target_pairs={{0,8},{8,0},{1,9},{9,1},{2,10},{10,2},{3,11},{11,3},{4,12},{12,4},... | collective-permute-start | bytes 460808 | tf_op jit(solution)/shard_map/ppermute | solution.py:533
  114.1 0.0 collective-permute-done.9.refs_1_
  114.1 0.0 copy-start.6
  114.1 0.0 collective-permute-done.10.refs_2_
  114.1 0.8 copy-done.6
  114.9 0.8 copy-done.7
  115.8 4.2 %expand_other.1 = bf16[192,240]{1,0:T(8,128)(2,1)} custom-call(bf16[80,4096]{1,0:T(8,128)(2,1)} %copy-done.5, bf16[80,4096]{1,0:T(8,128)(2,1)} %copy-done.6, bf16[80,4096]{1,0:T(8,128)(2,1)} %copy-done.7, bf16[192,4096]{1,0:T(8,128)(2,1)} %copy-done.4, bf16[192,4096]{1,0:T(8,128)(2,1)} %collective-permute-done.2.refs_4_.refs_6_), custom_call_target="tpu_custom_call" | custom-call | flops 754974720 | bytes 8388608 | tf_op jit(solution)/shard_map/expand_other/pallas_call | solution.py:150
  120.0 1.9 %collective-permute-start.11 = (bf16[192,240]{1,0:T(8,128)(2,1)}, bf16[192,240]{1,0:T(8,128)(2,1)S(1)}, u32[]{:S(2)}, u32[]{:S(2)}) collective-permute-start(bf16[192,240]{1,0:T(8,128)(2,1)} %expand_other.1), channel_id=1, source_target_pairs={{0,8},{8,0},{1,9},{9,1},{2,10},{10,2},{3,11},{11,3},{4,12},{12,4},... | collective-permute-start | bytes 276488 | tf_op jit(solution)/shard_map/ppermute | solution.py:533
  121.9 0.0 all-to-all-done.3.refs_2_
  121.9 0.0 copy-start.9
  121.9 0.7 copy-done.9
  122.6 5.4 %finish.1 = bf16[128,1024]{1,0:T(8,128)(2,1)} custom-call(s32[1]{0:T(128)} %bitcast.5.refs_0_, f32[32,128]{1,0:T(8,128)} %reduce_sum.9.refs_0_.refs_1_, bf16[8,160,128]{2,1,0:T(8,128)(2,1)} %copy-done.9, f32[128,128]{1,0:T(8,128)} %get-tuple-element.34.refs_3_.refs_2_, f32[128,128]{1,0:T(8,128)} %copy-done.2, f32[8,128]{1,0:T(8,128)} %copy-done.3, ...), custom_call_target="tpu_custom_call" | custom-call | flops 2147483648 | bytes 4194304 | tf_op jit(solution)/shard_map/finish/pallas_call | solution.py:58
  128.0 0.0 collective-permute-done.11.refs_7_
  128.0 0.0 copy-start.11
  128.0 0.0 collective-permute-done.12.refs_6_
  128.0 0.6 copy-done.11
  128.6 0.1 copy-done.10
  128.7 6.2 %last.1 = bf16[192,1280]{1,0:T(8,128)(2,1)} custom-call(s32[2]{0:T(128)} %pad_add_fusion.place_ref, bf16[80,4096]{1,0:T(8,128)(2,1)} %copy-done.5, bf16[80,4096]{1,0:T(8,128)(2,1)} %copy-done.6, bf16[80,4096]{1,0:T(8,128)(2,1)} %copy-done.7, bf16[192,4096]{1,0:T(8,128)(2,1)} %bitcast.12, bf16[192,4096]{1,0:T(8,128)(2,1)} %bitcast.15, ...), custom_call_target="tpu_custom_call" | custom-call | flops 1073741824 | bytes 8388608 | tf_op jit(solution)/shard_map/last/pallas_call | solution.py:233
  (8 shorter events, 0.0 us)
Async XLA Ops:
  0.6 35.8 %collective-permute-start.1 = (bf16[192,4096]{1,0:T(8,128)(2,1)}, bf16[192,4096]{1,0:T(8,128)(2,1)S(1)}, u32[]{:S(2)}, u32[]{:S(2)}) collective-permute-start(bf16[192,4096]{1,0:T(8,128)(2,1)} %bitcast.10), channel_id=1, source_target_pairs={{0,8},{8,0},{1,9},{9,1},{2,10},{10,2},{3,11},{11,3},{4,12},{12,4},... | collective-permute-start | bytes 4718600 | tf_op jit(solution)/shard_map/ppermute | solution.py:479
  9.4 27.0 %collective-permute-start.2 = (bf16[192,4096]{1,0:T(8,128)(2,1)}, bf16[192,4096]{1,0:T(8,128)(2,1)}, u32[]{:S(2)}, u32[]{:S(2)}) collective-permute-start(bf16[192,4096]{1,0:T(8,128)(2,1)} %bitcast.13), channel_id=1, source_target_pairs={{0,8},{8,0},{1,9},{9,1},{2,10},{10,2},{3,11},{11,3},{4,12},{12,4},... | collective-permute-start | bytes 4718600 | tf_op jit(solution)/shard_map/ppermute | solution.py:479
  13.5 23.0 %all-to-all-start = ((bf16[32,40,256]{2,1,0:T(8,128)(2,1)}), bf16[32,40,256]{2,1,0:T(8,128)(2,1)S(1)}, u32[]{:S(2)}, u32[]{:S(2)}) async-start(bf16[32,40,256]{2,1,0:T(8,128)(2,1)} %place.1), calls=%async_computation | async-start | bytes 1310720 | tf_op jit(solution)/shard_map/all_to_all | solution.py:448
  18.5 4.8 %collective-permute-start = (bf16[3,1024]{1,0:T(4,128)(2,1)S(1)}, bf16[3,1024]{1,0:T(4,128)(2,1)S(1)}, u32[]{:S(2)}, u32[]{:S(2)}) collective-permute-start(bf16[3,1024]{1,0:T(4,128)(2,1)S(1)} %slice.3), channel_id=1, source_target_pairs={{0,8},{8,16},{16,24},{24,32},{32,40},{40,48},{48,56},{56,64},{64,7... | collective-permute-start | bytes 18440 | tf_op jit(solution)/shard_map/ppermute | solution.py:437
  23.4 0.6 copy-start.12
  36.5 37.6 %copy-start.4 = (bf16[192,4096]{1,0:T(8,128)(2,1)}, bf16[192,4096]{1,0:T(8,128)(2,1)S(1)}, u32[]{:S(2)}) copy-start(bf16[192,4096]{1,0:T(8,128)(2,1)S(1)} %collective-permute-done.1.refs_3_.refs_5_) | copy-start | bytes 4718596
  37.1 37.0 %copy-start = (bf16[80,4096]{1,0:T(8,128)(2,1)}, bf16[80,4096]{1,0:T(8,128)(2,1)S(1)}, u32[]{:S(2)}) copy-start(bf16[80,4096]{1,0:T(8,128)(2,1)S(1)} %assemble.1.refs_0_) | copy-start | bytes 1966084
  37.1 15.2 %collective-permute-start.4 = (bf16[80,4096]{1,0:T(8,128)(2,1)S(1)}, bf16[80,4096]{1,0:T(8,128)(2,1)}, u32[]{:S(2)}, u32[]{:S(2)}) collective-permute-start(bf16[80,4096]{1,0:T(8,128)(2,1)S(1)} %assemble.1.refs_0_), channel_id=1, source_target_pairs={{0,8},{8,0},{1,9},{9,1},{2,10},{10,2},{3,11},{11,3},{4,12},{12,4},... | collective-permute-start | bytes 1966088 | tf_op jit(solution)/shard_map/ppermute | solution.py:496
  41.6 18.2 %collective-permute-start.3 = (bf16[80,4096]{1,0:T(8,128)(2,1)S(1)}, bf16[80,4096]{1,0:T(8,128)(2,1)S(1)}, u32[]{:S(2)}, u32[]{:S(2)}) collective-permute-start(bf16[80,4096]{1,0:T(8,128)(2,1)S(1)} %assemble.1.refs_0_), channel_id=1, source_target_pairs={{0,64},{8,456},{64,128},{72,8},{128,192},{136,72},{192,256},{200,1... | collective-permute-start | bytes 1966088 | tf_op jit(solution)/shard_map/ppermute | solution.py:494
  52.3 11.2 %all-to-all-start.1 = ((f32[8,32,128]{2,1,0:T(8,128)}), f32[8,32,128]{2,1,0:T(8,128)S(1)}, u32[]{:S(2)}, u32[]{:S(2)}) async-start(f32[8,32,128]{2,1,0:T(8,128)} %get-tuple-element.29), calls=%async_computation.1 | async-start | bytes 262144 | tf_op jit(solution)/shard_map/all_to_all | solution.py:499
  55.7 18.4 %collective-permute-start.7 = (bf16[80,4096]{1,0:T(8,128)(2,1)}, bf16[80,4096]{1,0:T(8,128)(2,1)}, u32[]{:S(2)}, u32[]{:S(2)}) collective-permute-start(bf16[80,4096]{1,0:T(8,128)(2,1)} %collective-permute-done.4), channel_id=1, source_target_pairs={{0,64},{8,456},{64,128},{72,8},{128,192},{136,72},{192,256},{200,1... | collective-permute-start | bytes 1966088 | tf_op jit(solution)/shard_map/ppermute | solution.py:494
  59.8 14.3 %copy-start.8 = (bf16[80,4096]{1,0:T(8,128)(2,1)}, bf16[80,4096]{1,0:T(8,128)(2,1)S(1)}, u32[]{:S(2)}) copy-start(bf16[80,4096]{1,0:T(8,128)(2,1)S(1)} %collective-permute-done.3.refs_1_) | copy-start | bytes 1966084
  63.5 12.5 %collective-permute-start.5 = (bf16[80,4096]{1,0:T(8,128)(2,1)S(1)}, bf16[80,4096]{1,0:T(8,128)(2,1)}, u32[]{:S(2)}, u32[]{:S(2)}) collective-permute-start(bf16[80,4096]{1,0:T(8,128)(2,1)S(1)} %collective-permute-done.3.refs_1_), channel_id=1, source_target_pairs={{0,64},{8,456},{64,128},{72,8},{128,192},{136,72},{192,256},{200,1... | collective-permute-start | bytes 1966088 | tf_op jit(solution)/shard_map/ppermute | solution.py:494
  67.0 28.8 %copy-start.1 = (f32[128,128]{1,0:T(8,128)S(1)}, f32[128,128]{1,0:T(8,128)}, u32[]{:S(2)}) copy-start(f32[128,128]{1,0:T(8,128)} %get-tuple-element.34.refs_3_.refs_2_) | copy-start | bytes 196612
  74.1 11.9 %collective-permute-start.8 = (bf16[80,4096]{1,0:T(8,128)(2,1)}, bf16[80,4096]{1,0:T(8,128)(2,1)}, u32[]{:S(2)}, u32[]{:S(2)}) collective-permute-start(bf16[80,4096]{1,0:T(8,128)(2,1)} %collective-permute-done.7.refs_2_), channel_id=1, source_target_pairs={{0,64},{8,456},{64,128},{72,8},{128,192},{136,72},{192,256},{200,1... | collective-permute-start | bytes 1966088 | tf_op jit(solution)/shard_map/ppermute | solution.py:494
  76.0 16.9 %collective-permute-start.6 = (bf16[80,4096]{1,0:T(8,128)(2,1)}, bf16[80,4096]{1,0:T(8,128)(2,1)S(1)}, u32[]{:S(2)}, u32[]{:S(2)}) collective-permute-start(bf16[80,4096]{1,0:T(8,128)(2,1)} %collective-permute-done.5.refs_3_), channel_id=1, source_target_pairs={{0,64},{8,456},{64,128},{72,8},{128,192},{136,72},{192,256},{200,1... | collective-permute-start | bytes 1966088 | tf_op jit(solution)/shard_map/ppermute | solution.py:494
  79.1 16.7 %all-to-all-start.2 = ((bf16[8,160,128]{2,1,0:T(8,128)(2,1)}), bf16[8,160,128]{2,1,0:T(8,128)(2,1)S(1)}, u32[]{:S(2)}, u32[]{:S(2)}) async-start(bf16[8,160,128]{2,1,0:T(8,128)(2,1)} %get-tuple-element.35), calls=%async_computation.2 | async-start | bytes 655360 | tf_op jit(solution)/shard_map/all_to_all | solution.py:512
  86.0 28.1 %collective-permute-start.9 = (bf16[80,4096]{1,0:T(8,128)(2,1)}, bf16[80,4096]{1,0:T(8,128)(2,1)S(1)}, u32[]{:S(2)}, u32[]{:S(2)}) collective-permute-start(bf16[80,4096]{1,0:T(8,128)(2,1)} %collective-permute-done.8.refs_4_), channel_id=1, source_target_pairs={{0,64},{8,456},{64,128},{72,8},{128,192},{136,72},{192,256},{200,1... | collective-permute-start | bytes 1966088 | tf_op jit(solution)/shard_map/ppermute | solution.py:494
  92.9 16.1 %copy-start.5 = (bf16[80,4096]{1,0:T(8,128)(2,1)}, bf16[80,4096]{1,0:T(8,128)(2,1)S(1)}, u32[]{:S(2)}) copy-start(bf16[80,4096]{1,0:T(8,128)(2,1)S(1)} %collective-permute-done.6.refs_0_) | copy-start | bytes 1966084
  92.9 21.2 %collective-permute-start.10 = (bf16[80,4096]{1,0:T(8,128)(2,1)S(1)}, bf16[80,4096]{1,0:T(8,128)(2,1)S(1)}, u32[]{:S(2)}, u32[]{:S(2)}) collective-permute-start(bf16[80,4096]{1,0:T(8,128)(2,1)S(1)} %collective-permute-done.6.refs_0_), channel_id=1, source_target_pairs={{0,64},{8,456},{64,128},{72,8},{128,192},{136,72},{192,256},{200,1... | collective-permute-start | bytes 1966088 | tf_op jit(solution)/shard_map/ppermute | solution.py:494
  97.1 0.6 copy-start.2
  97.7 11.4 %copy-start.3 = (f32[8,128]{1,0:T(8,128)}, f32[8,128]{1,0:T(8,128)S(1)}, u32[]{:S(2)}) copy-start(f32[8,128]{1,0:T(8,128)S(1)} %get-tuple-element.42.refs_5_) | copy-start | bytes 12292
  97.7 24.2 %all-to-all-start.3 = ((bf16[8,160,128]{2,1,0:T(8,128)(2,1)}), bf16[8,160,128]{2,1,0:T(8,128)(2,1)S(1)}, u32[]{:S(2)}, u32[]{:S(2)}) async-start(bf16[8,160,128]{2,1,0:T(8,128)(2,1)} %get-tuple-element.40), calls=%async_computation.3 | async-start | bytes 655360 | tf_op jit(solution)/shard_map/all_to_all | solution.py:520
  109.1 18.9 %collective-permute-start.12 = (bf16[192,400]{1,0:T(8,128)(2,1)}, bf16[192,400]{1,0:T(8,128)(2,1)S(1)}, u32[]{:S(2)}, u32[]{:S(2)}) collective-permute-start(bf16[192,400]{1,0:T(8,128)(2,1)} %get-tuple-element.48), channel_id=1, source_target_pairs={{0,8},{8,0},{1,9},{9,1},{2,10},{10,2},{3,11},{11,3},{4,12},{12,4},... | collective-permute-start | bytes 460808 | tf_op jit(solution)/shard_map/ppermute | solution.py:533
  114.1 0.8 copy-start.6
  114.9 0.9 copy-start.7
  120.0 8.0 %collective-permute-start.11 = (bf16[192,240]{1,0:T(8,128)(2,1)}, bf16[192,240]{1,0:T(8,128)(2,1)S(1)}, u32[]{:S(2)}, u32[]{:S(2)}) collective-permute-start(bf16[192,240]{1,0:T(8,128)(2,1)} %expand_other.1), channel_id=1, source_target_pairs={{0,8},{8,0},{1,9},{9,1},{2,10},{10,2},{3,11},{11,3},{4,12},{12,4},... | collective-permute-start | bytes 276488 | tf_op jit(solution)/shard_map/ppermute | solution.py:533
  121.9 0.7 copy-start.9
  128.0 0.6 copy-start.11
  128.0 0.7 copy-start.10

commit v3 on v2

--- a/solution.py
+++ b/solution.py
@@ -508,6 +508,8 @@
     own[2], _ = lax.optimization_barrier((own[2], ends))
     own.append(step_on(own[2]))
     twin.append(step_on(twin[2]))
+    other_early, mine_early = expand([block, own[1], twin[1], own[2], twin[2]], pairs, "expand_early")
+    own[3], _ = lax.optimization_barrier((own[3], other_early))
     own.append(step_on(own[3]))
     near = lax.all_to_all(ends, ("x", "c"), split_axis=0, concat_axis=0, tiled=True)
     place_in = lax.axis_index(("x", "c")).astype(jnp.int32).reshape(1)
@@ -527,7 +529,6 @@
         lazy=True, name="finish", flops=1 << 31,
     )(layer, coef, far, rate, before, before_step, local, sums, conv, skip_gain[None], inner_z)
 
-    other_early, mine_early = expand([block, own[1], twin[1], own[2], twin[2]], pairs, "expand_early")
     late = [own[3], twin[3], own[4]]
     (other_late,) = expand(late, pairs[:1], "expand_other")
     other_early, other_late = (lax.ppermute(part, "c", swap) for part in (other_early, other_late))

time: 136 us -> 137 us (level)
  waiting for transfers between devices: 21.3 us -> 19.8 us
    ppermute x7, waiting for transfers between devices: 8.08 us -> 1.93 us  [step_on(): return lax.ppermute(rows, ('z', 'c'), onward)]
    ppermute x2, starting transfers between devices: 6.89 us -> 4.31 us  [shards(): lax.ppermute(part, 'c', swap)]
    all_to_all x1, waiting for transfers between devices: 0.01 us -> 2.45 us  [shards(): far = lax.all_to_all(whole, 'z', split_axis=0, concat_axis=0, tiled=True)]
    all_to_all x1, waiting for transfers between devices: 3.73 us -> 5.92 us  [shards(): coef = lax.all_to_all(part, 'exp', split_axis=0, concat_axis=0, tiled=True)]
    all_to_all x1, starting transfers between devices: 3.43 us -> 5.46 us  [shards(): far = lax.all_to_all(whole, 'z', split_axis=0, concat_axis=0, tiled=True)]
    unnamed x26 -> x32, local copies, waits for them, and re-layouts: 4.31 us -> 4.92 us
  transfers between devices with their start and end apart: 17 -> 17, of which waited for: 6 -> 5; matrix products, arithmetic and copies ran while one was open for 1% -> 2% of each run, Pallas kernels for 23% -> 23%
where the time goes in v3:
time: 137 us; the launch traced here: 135 us
  starting transfers between devices  69.1 us (50%)
  Pallas kernels  37.7 us (28%)
  waiting for transfers between devices  19.8 us (14%)
  local copies, waits for them, and re-layouts  5.64 us (4%)
  other arithmetic  2.11 us (2%)
    ppermute x7, starting transfers between devices, step_on(): return lax.ppermute(rows, ('z', 'c'), onward)  26.5 us
    pallas_call x6, Pallas kernels, run(): pl.pallas_call(body, out_shape=outs, in_specs=in_specs, out_specs=(WHOLE,...  20 us
    pallas_call x2, Pallas kernels, expand(): pl.pallas_call(functools.partial(expand_kernel, len(blocks), total), out_...  11.5 us
    ppermute x2, starting transfers between devices, shards(): others = [lax.ppermute(weight, 'c', swap) for weight in weights]  10.7 us
    all_to_all x1, waiting for transfers between devices, shards(): lax.all_to_all(placed, ('exp', 'x'), split_axis=0, concat_axis=0, tiled=T...  8.7 us
    pallas_call x1, Pallas kernels, last(): pl.pallas_call(last_kernel, out_shape=out, in_specs=[SMEM] + [WHOLE] * 8,...  6.25 us
    all_to_all x1, waiting for transfers between devices, shards(): coef = lax.all_to_all(part, 'exp', split_axis=0, concat_axis=0, tiled=True)  5.92 us
    all_to_all x1, starting transfers between devices, shards(): lax.all_to_all(ends, ('x', 'c'), split_axis=0, concat_axis=0, tiled=True)  5.83 us
  transfers between devices with their start and end apart: 17, of which 5 were waited for; matrix products, arithmetic and copies ran while one was open for 2% of the time, Pallas kernels for 23%

profile of v3, /device:TPU:1, one launch (start us, length us, event | category | flops | bytes accessed | tf_op | source)
XLA Modules:
  0.0 135.4 jit_solution(17034951521976557996)
XLA Ops:
  0.6 8.8 %collective-permute-start.1 = (bf16[192,4096]{1,0:T(8,128)(2,1)}, bf16[192,4096]{1,0:T(8,128)(2,1)S(1)}, u32[]{:S(2)}, u32[]{:S(2)}) collective-permute-start(bf16[192,4096]{1,0:T(8,128)(2,1)} %bitcast.10), channel_id=1, source_target_pairs={{0,8},{8,0},{1,9},{9,1},{2,10},{10,2},{3,11},{11,3},{4,12},{12,4},... | collective-permute-start | bytes 4718600 | tf_op jit(solution)/shard_map/ppermute | solution.py:479
  9.4 1.9 %collective-permute-start.2 = (bf16[192,4096]{1,0:T(8,128)(2,1)}, bf16[192,4096]{1,0:T(8,128)(2,1)}, u32[]{:S(2)}, u32[]{:S(2)}) collective-permute-start(bf16[192,4096]{1,0:T(8,128)(2,1)} %bitcast.13), channel_id=1, source_target_pairs={{0,8},{8,0},{1,9},{9,1},{2,10},{10,2},{3,11},{11,3},{4,12},{12,4},... | collective-permute-start | bytes 4718600 | tf_op jit(solution)/shard_map/ppermute | solution.py:479
  11.4 2.1 %place.1 = bf16[32,40,256]{2,1,0:T(8,128)(2,1)} custom-call(s32[2,128]{1,0:T(2,128)} %bitcast.20, bf16[128,512]{1,0:T(8,128)(2,1)} %refs_1_.1), custom_call_target="tpu_custom_call" | custom-call | flops 268435456 | bytes 4194304 | tf_op jit(solution)/shard_map/place/pallas_call | solution.py:58
  13.5 4.3 %all-to-all-start = ((bf16[32,40,256]{2,1,0:T(8,128)(2,1)}), bf16[32,40,256]{2,1,0:T(8,128)(2,1)S(1)}, u32[]{:S(2)}, u32[]{:S(2)}) async-start(bf16[32,40,256]{2,1,0:T(8,128)(2,1)} %place.1), calls=%async_computation | async-start | bytes 1310720 | tf_op jit(solution)/shard_map/all_to_all | solution.py:448
  17.8 0.7 slice.3
  18.5 4.1 %collective-permute-start = (bf16[3,1024]{1,0:T(4,128)(2,1)S(1)}, bf16[3,1024]{1,0:T(4,128)(2,1)S(1)}, u32[]{:S(2)}, u32[]{:S(2)}) collective-permute-start(bf16[3,1024]{1,0:T(4,128)(2,1)S(1)} %slice.3), channel_id=1, source_target_pairs={{0,8},{8,16},{16,24},{24,32},{32,40},{40,48},{48,56},{56,64},{64,7... | collective-permute-start | bytes 18440 | tf_op jit(solution)/shard_map/ppermute | solution.py:437
  22.6 0.8 collective-permute-done.refs_1_
  23.4 0.6 copy-done.15
  24.0 3.8 %conv.1 = (f32[128,1024]{1,0:T(8,128)}, f32[1024,128]{1,0:T(8,128)}, f32[1024,128]{1,0:T(8,128)}, f32[128,128]{1,0:T(8,128)}, f32[8,32,128]{2,1,0:T(8,128)}) custom-call(bf16[128,1024]{1,0:T(8,128)(2,1)} %refs_0_.1, bf16[3,1024]{1,0:T(4,128)(2,1)} %copy-done.15, bf16[128,1024]{1,0:T(8,128)(2,1)} %refs_2_.1, f32[4,1024]{1,0:T(4,128)} %refs_3_.1, ...), custom_call_target="tpu_custom_call" | custom-call | flops 536870912 | bytes 4194304 | tf_op jit(solution)/shard_map/conv/pallas_call | solution.py:58
  27.7 8.7 %all-to-all-done.refs_0_ = bf16[32,40,256]{2,1,0:T(8,128)(2,1)S(1)} async-done(((bf16[32,40,256]{2,1,0:T(8,128)(2,1)}), bf16[32,40,256]{2,1,0:T(8,128)(2,1)S(1)}, u32[]{:S(2)}, u32[]{:S(2)}) %all-to-all-start) | async-done | bytes 655392 | tf_op jit(solution)/shard_map/all_to_all | solution.py:448
  36.5 0.0 collective-permute-done.1.refs_5_.refs_3_
  36.5 0.0 collective-permute-done.2.refs_6_.refs_4_
  36.5 0.6 assemble.1.refs_0_
  37.0 0.0 copy-start
  37.1 4.5 %collective-permute-start.4 = (bf16[80,4096]{1,0:T(8,128)(2,1)S(1)}, bf16[80,4096]{1,0:T(8,128)(2,1)}, u32[]{:S(2)}, u32[]{:S(2)}) collective-permute-start(bf16[80,4096]{1,0:T(8,128)(2,1)S(1)} %assemble.1.refs_0_), channel_id=1, source_target_pairs={{0,8},{8,0},{1,9},{9,1},{2,10},{10,2},{3,11},{11,3},{4,12},{12,4},... | collective-permute-start | bytes 1966088 | tf_op jit(solution)/shard_map/ppermute | solution.py:496
  41.6 10.7 %collective-permute-start.3 = (bf16[80,4096]{1,0:T(8,128)(2,1)S(1)}, bf16[80,4096]{1,0:T(8,128)(2,1)S(1)}, u32[]{:S(2)}, u32[]{:S(2)}) collective-permute-start(bf16[80,4096]{1,0:T(8,128)(2,1)S(1)} %assemble.1.refs_0_), channel_id=1, source_target_pairs={{0,64},{8,456},{64,128},{72,8},{128,192},{136,72},{192,256},{200,1... | collective-permute-start | bytes 1966088 | tf_op jit(solution)/shard_map/ppermute | solution.py:494
  52.3 0.0 collective-permute-done.4
  52.3 2.2 %collective-permute-start.7 = (bf16[80,4096]{1,0:T(8,128)(2,1)}, bf16[80,4096]{1,0:T(8,128)(2,1)}, u32[]{:S(2)}, u32[]{:S(2)}) collective-permute-start(bf16[80,4096]{1,0:T(8,128)(2,1)} %collective-permute-done.4), channel_id=1, source_target_pairs={{0,64},{8,456},{64,128},{72,8},{128,192},{136,72},{192,256},{200,1... | collective-permute-start | bytes 1966088 | tf_op jit(solution)/shard_map/ppermute | solution.py:494
  54.5 3.4 %all-to-all-start.1 = ((f32[8,32,128]{2,1,0:T(8,128)}), f32[8,32,128]{2,1,0:T(8,128)S(1)}, u32[]{:S(2)}, u32[]{:S(2)}) async-start(f32[8,32,128]{2,1,0:T(8,128)} %get-tuple-element.30), calls=%async_computation.1 | async-start | bytes 262144 | tf_op jit(solution)/shard_map/all_to_all | solution.py:499
  57.9 1.9 %collective-permute-done.3.refs_1_ = bf16[80,4096]{1,0:T(8,128)(2,1)S(1)} collective-permute-done((bf16[80,4096]{1,0:T(8,128)(2,1)S(1)}, bf16[80,4096]{1,0:T(8,128)(2,1)S(1)}, u32[]{:S(2)}, u32[]{:S(2)}) %collective-permute-start.3) | collective-permute-done | bytes 655392 | tf_op jit(solution)/shard_map/ppermute | solution.py:494
  59.8 5.9 %all-to-all-done.1 = f32[8,32,128]{2,1,0:T(8,128)S(1)} async-done(((f32[8,32,128]{2,1,0:T(8,128)}), f32[8,32,128]{2,1,0:T(8,128)S(1)}, u32[]{:S(2)}, u32[]{:S(2)}) %all-to-all-start.1) | async-done | bytes 131104 | tf_op jit(solution)/shard_map/all_to_all | solution.py:499
  65.7 3.8 %collective-permute-start.5 = (bf16[80,4096]{1,0:T(8,128)(2,1)S(1)}, bf16[80,4096]{1,0:T(8,128)(2,1)}, u32[]{:S(2)}, u32[]{:S(2)}) collective-permute-start(bf16[80,4096]{1,0:T(8,128)(2,1)S(1)} %collective-permute-done.3.refs_1_), channel_id=1, source_target_pairs={{0,64},{8,456},{64,128},{72,8},{128,192},{136,72},{192,256},{200,1... | collective-permute-start | bytes 1966088 | tf_op jit(solution)/shard_map/ppermute | solution.py:494
  69.6 0.0 copy-done.10
  69.6 0.0 collective-permute-done.7.refs_2_
  69.6 2.3 %collective-permute-start.8 = (bf16[80,4096]{1,0:T(8,128)(2,1)}, bf16[80,4096]{1,0:T(8,128)(2,1)S(1)}, u32[]{:S(2)}, u32[]{:S(2)}) collective-permute-start(bf16[80,4096]{1,0:T(8,128)(2,1)} %collective-permute-done.7.refs_2_), channel_id=1, source_target_pairs={{0,64},{8,456},{64,128},{72,8},{128,192},{136,72},{192,256},{200,1... | collective-permute-start | bytes 1966088 | tf_op jit(solution)/shard_map/ppermute | solution.py:494
  71.9 1.5 %reduce_sum.9.refs_0_.refs_1_ = f32[32,128]{1,0:T(8,128)} reduce(f32[8,32,128]{2,1,0:T(8,128)} %copy-done.10, f32[]{:T(128)} %constant.6.clone.1), dimensions={0}, to_apply=%region_0.0 | reduce | flops 28672 | bytes 147460 | tf_op jit(solution)/shard_map/reduce_sum | solution.py:501
  73.5 6.9 %scan.1 = (f32[1024,128]{1,0:T(8,128)}, f32[1024,128]{1,0:T(8,128)}, bf16[8,160,128]{2,1,0:T(8,128)(2,1)}) custom-call(f32[32,128]{1,0:T(8,128)} %reduce_sum.9.refs_0_.refs_1_, f32[1024,128]{1,0:T(8,128)} %get-tuple-element.33.refs_1_, f32[1024,128]{1,0:T(8,128)} %get-tuple-element.34.refs_2_, f32[128,128]{1,0:T(8,128)} %get-tuple-element.35.refs_3_.refs_2_), custom_call_target="tpu_custom_call" | custom-call | flops 2147483648 | bytes 4194304 | tf_op jit(solution)/shard_map/scan/pallas_call | solution.py:58
  80.3 0.0 copy-done.4
  80.4 0.0 copy-done
  80.4 0.0 copy-done.9
  80.4 0.0 collective-permute-done.5.refs_3_
  80.4 1.9 %collective-permute-start.6 = (bf16[80,4096]{1,0:T(8,128)(2,1)}, bf16[80,4096]{1,0:T(8,128)(2,1)S(1)}, u32[]{:S(2)}, u32[]{:S(2)}) collective-permute-start(bf16[80,4096]{1,0:T(8,128)(2,1)} %collective-permute-done.5.refs_3_), channel_id=1, source_target_pairs={{0,64},{8,456},{64,128},{72,8},{128,192},{136,72},{192,256},{200,1... | collective-permute-start | bytes 1966088 | tf_op jit(solution)/shard_map/ppermute | solution.py:494
  82.3 5.8 %all-to-all-start.2 = ((bf16[8,160,128]{2,1,0:T(8,128)(2,1)}), bf16[8,160,128]{2,1,0:T(8,128)(2,1)S(1)}, u32[]{:S(2)}, u32[]{:S(2)}) async-start(bf16[8,160,128]{2,1,0:T(8,128)(2,1)} %get-tuple-element.36), calls=%async_computation.2 | async-start | bytes 655360 | tf_op jit(solution)/shard_map/all_to_all | solution.py:514
  88.1 0.0 collective-permute-done.8.refs_4_
  88.1 0.0 copy-start.8
  88.2 3.5 %collective-permute-start.9 = (bf16[80,4096]{1,0:T(8,128)(2,1)S(1)}, bf16[80,4096]{1,0:T(8,128)(2,1)S(1)}, u32[]{:S(2)}, u32[]{:S(2)}) collective-permute-start(bf16[80,4096]{1,0:T(8,128)(2,1)S(1)} %collective-permute-done.8.refs_4_), channel_id=1, source_target_pairs={{0,64},{8,456},{64,128},{72,8},{128,192},{136,72},{192,256},{200,1... | collective-permute-start | bytes 1966088 | tf_op jit(solution)/shard_map/ppermute | solution.py:494
  91.7 0.0 copy-done.8
  91.7 7.3 %expand_early.1 = (bf16[192,400]{1,0:T(8,128)(2,1)}, bf16[192,400]{1,0:T(8,128)(2,1)}) custom-call(bf16[80,4096]{1,0:T(8,128)(2,1)} %copy-done, bf16[80,4096]{1,0:T(8,128)(2,1)} %copy-done.9, bf16[80,4096]{1,0:T(8,128)(2,1)} %collective-permute-done.7.refs_2_, bf16[80,4096]{1,0:T(8,128)(2,1)} %collective-permute-done.5.refs_3_, bf16[80,4096]{1,0:T(8,128)(2,1)} %copy-done.8, ...), custom_call_target="tpu_custom_call" | custom-call | flops 2516582400 | bytes 8388608 | tf_op jit(solution)/shard_map/expand_early/pallas_call | solution.py:150
  99.0 0.0 copy-start.14
  99.0 0.0 collective-permute-done.6.refs_0_
  99.0 2.1 %collective-permute-start.10 = (bf16[80,4096]{1,0:T(8,128)(2,1)S(1)}, bf16[80,4096]{1,0:T(8,128)(2,1)S(1)}, u32[]{:S(2)}, u32[]{:S(2)}) collective-permute-start(bf16[80,4096]{1,0:T(8,128)(2,1)S(1)} %collective-permute-done.6.refs_0_), channel_id=1, source_target_pairs={{0,64},{8,456},{64,128},{72,8},{128,192},{136,72},{192,256},{200,1... | collective-permute-start | bytes 1966088 | tf_op jit(solution)/shard_map/ppermute | solution.py:494
  101.1 0.0 all-to-all-done.2.refs_1_
  101.1 0.0 copy-done.1
  101.1 1.3 group.1
  102.4 0.6 copy-done.2
  103.0 0.6 copy-done.3
  103.6 5.5 %all-to-all-start.3 = ((bf16[8,160,128]{2,1,0:T(8,128)(2,1)}), bf16[8,160,128]{2,1,0:T(8,128)(2,1)S(1)}, u32[]{:S(2)}, u32[]{:S(2)}) async-start(bf16[8,160,128]{2,1,0:T(8,128)(2,1)} %get-tuple-element.43), calls=%async_computation.3 | async-start | bytes 655360 | tf_op jit(solution)/shard_map/all_to_all | solution.py:522
  109.1 0.6 pad_add_fusion.place_ref
  109.7 1.9 %collective-permute-start.12 = (bf16[192,400]{1,0:T(8,128)(2,1)S(1)}, bf16[192,400]{1,0:T(8,128)(2,1)S(1)}, u32[]{:S(2)}, u32[]{:S(2)}) collective-permute-start(bf16[192,400]{1,0:T(8,128)(2,1)S(1)} %copy-done.14), channel_id=1, source_target_pairs={{0,8},{8,0},{1,9},{9,1},{2,10},{10,2},{3,11},{11,3},{4,12},{12,4},... | collective-permute-start | bytes 460808 | tf_op jit(solution)/shard_map/ppermute | solution.py:534
  111.6 0.0 collective-permute-done.9.refs_1_
  111.6 0.0 collective-permute-done.10.refs_2_
  111.6 0.8 copy-done.6
  112.4 0.8 copy-done.7
  113.3 4.2 %expand_other.1 = bf16[192,240]{1,0:T(8,128)(2,1)} custom-call(bf16[80,4096]{1,0:T(8,128)(2,1)} %copy-done.5, bf16[80,4096]{1,0:T(8,128)(2,1)} %copy-done.6, bf16[80,4096]{1,0:T(8,128)(2,1)} %copy-done.7, bf16[192,4096]{1,0:T(8,128)(2,1)} %copy-done.4, bf16[192,4096]{1,0:T(8,128)(2,1)} %collective-permute-done.2.refs_6_.refs_4_), custom_call_target="tpu_custom_call" | custom-call | flops 754974720 | bytes 8388608 | tf_op jit(solution)/shard_map/expand_other/pallas_call | solution.py:150
  117.4 2.4 %collective-permute-start.11 = (bf16[192,240]{1,0:T(8,128)(2,1)}, bf16[192,240]{1,0:T(8,128)(2,1)S(1)}, u32[]{:S(2)}, u32[]{:S(2)}) collective-permute-start(bf16[192,240]{1,0:T(8,128)(2,1)} %expand_other.1), channel_id=1, source_target_pairs={{0,8},{8,0},{1,9},{9,1},{2,10},{10,2},{3,11},{11,3},{4,12},{12,4},... | collective-permute-start | bytes 276488 | tf_op jit(solution)/shard_map/ppermute | solution.py:534
  119.9 2.4 %all-to-all-done.3.refs_2_ = bf16[8,160,128]{2,1,0:T(8,128)(2,1)S(1)} async-done(((bf16[8,160,128]{2,1,0:T(8,128)(2,1)}), bf16[8,160,128]{2,1,0:T(8,128)(2,1)S(1)}, u32[]{:S(2)}, u32[]{:S(2)}) %all-to-all-start.3) | async-done | bytes 327712 | tf_op jit(solution)/shard_map/all_to_all | solution.py:522
  122.3 0.7 copy-done.11
  123.0 5.4 %finish.1 = bf16[128,1024]{1,0:T(8,128)(2,1)} custom-call(s32[1]{0:T(128)} %bitcast.5.refs_0_, f32[32,128]{1,0:T(8,128)} %reduce_sum.9.refs_0_.refs_1_, bf16[8,160,128]{2,1,0:T(8,128)(2,1)} %copy-done.11, f32[128,128]{1,0:T(8,128)} %get-tuple-element.35.refs_3_.refs_2_, f32[128,128]{1,0:T(8,128)} %copy-done.2, f32[8,128]{1,0:T(8,128)} %copy-done.3, ...), custom_call_target="tpu_custom_call" | custom-call | flops 2147483648 | bytes 4194304 | tf_op jit(solution)/shard_map/finish/pallas_call | solution.py:58
  128.4 0.0 collective-permute-done.11.refs_7_
  128.4 0.0 collective-permute-done.12.refs_6_
  128.4 0.0 copy-start.12
  128.4 0.6 copy-done.13
  129.0 0.1 copy-done.12
  129.1 6.2 %last.1 = bf16[192,1280]{1,0:T(8,128)(2,1)} custom-call(s32[2]{0:T(128)} %pad_add_fusion.place_ref, bf16[80,4096]{1,0:T(8,128)(2,1)} %copy-done.5, bf16[80,4096]{1,0:T(8,128)(2,1)} %copy-done.6, bf16[80,4096]{1,0:T(8,128)(2,1)} %copy-done.7, bf16[192,4096]{1,0:T(8,128)(2,1)} %bitcast.12, bf16[192,4096]{1,0:T(8,128)(2,1)} %bitcast.15, ...), custom_call_target="tpu_custom_call" | custom-call | flops 1073741824 | bytes 8388608 | tf_op jit(solution)/shard_map/last/pallas_call | solution.py:233
  (14 shorter events, 0.0 us)
Async XLA Ops:
  0.6 35.8 %collective-permute-start.1 = (bf16[192,4096]{1,0:T(8,128)(2,1)}, bf16[192,4096]{1,0:T(8,128)(2,1)S(1)}, u32[]{:S(2)}, u32[]{:S(2)}) collective-permute-start(bf16[192,4096]{1,0:T(8,128)(2,1)} %bitcast.10), channel_id=1, source_target_pairs={{0,8},{8,0},{1,9},{9,1},{2,10},{10,2},{3,11},{11,3},{4,12},{12,4},... | collective-permute-start | bytes 4718600 | tf_op jit(solution)/shard_map/ppermute | solution.py:479
  9.4 27.0 %collective-permute-start.2 = (bf16[192,4096]{1,0:T(8,128)(2,1)}, bf16[192,4096]{1,0:T(8,128)(2,1)}, u32[]{:S(2)}, u32[]{:S(2)}) collective-permute-start(bf16[192,4096]{1,0:T(8,128)(2,1)} %bitcast.13), channel_id=1, source_target_pairs={{0,8},{8,0},{1,9},{9,1},{2,10},{10,2},{3,11},{11,3},{4,12},{12,4},... | collective-permute-start | bytes 4718600 | tf_op jit(solution)/shard_map/ppermute | solution.py:479
  13.5 23.0 %all-to-all-start = ((bf16[32,40,256]{2,1,0:T(8,128)(2,1)}), bf16[32,40,256]{2,1,0:T(8,128)(2,1)S(1)}, u32[]{:S(2)}, u32[]{:S(2)}) async-start(bf16[32,40,256]{2,1,0:T(8,128)(2,1)} %place.1), calls=%async_computation | async-start | bytes 1310720 | tf_op jit(solution)/shard_map/all_to_all | solution.py:448
  18.5 4.8 %collective-permute-start = (bf16[3,1024]{1,0:T(4,128)(2,1)S(1)}, bf16[3,1024]{1,0:T(4,128)(2,1)S(1)}, u32[]{:S(2)}, u32[]{:S(2)}) collective-permute-start(bf16[3,1024]{1,0:T(4,128)(2,1)S(1)} %slice.3), channel_id=1, source_target_pairs={{0,8},{8,16},{16,24},{24,32},{32,40},{40,48},{48,56},{56,64},{64,7... | collective-permute-start | bytes 18440 | tf_op jit(solution)/shard_map/ppermute | solution.py:437
  23.4 0.6 copy-start.15
  36.5 43.9 %copy-start.4 = (bf16[192,4096]{1,0:T(8,128)(2,1)}, bf16[192,4096]{1,0:T(8,128)(2,1)S(1)}, u32[]{:S(2)}) copy-start(bf16[192,4096]{1,0:T(8,128)(2,1)S(1)} %collective-permute-done.1.refs_5_.refs_3_) | copy-start | bytes 4718596
  37.0 43.3 %copy-start = (bf16[80,4096]{1,0:T(8,128)(2,1)}, bf16[80,4096]{1,0:T(8,128)(2,1)S(1)}, u32[]{:S(2)}) copy-start(bf16[80,4096]{1,0:T(8,128)(2,1)S(1)} %assemble.1.refs_0_) | copy-start | bytes 1966084
  37.1 15.2 %collective-permute-start.4 = (bf16[80,4096]{1,0:T(8,128)(2,1)S(1)}, bf16[80,4096]{1,0:T(8,128)(2,1)}, u32[]{:S(2)}, u32[]{:S(2)}) collective-permute-start(bf16[80,4096]{1,0:T(8,128)(2,1)S(1)} %assemble.1.refs_0_), channel_id=1, source_target_pairs={{0,8},{8,0},{1,9},{9,1},{2,10},{10,2},{3,11},{11,3},{4,12},{12,4},... | collective-permute-start | bytes 1966088 | tf_op jit(solution)/shard_map/ppermute | solution.py:496
  41.6 18.2 %collective-permute-start.3 = (bf16[80,4096]{1,0:T(8,128)(2,1)S(1)}, bf16[80,4096]{1,0:T(8,128)(2,1)S(1)}, u32[]{:S(2)}, u32[]{:S(2)}) collective-permute-start(bf16[80,4096]{1,0:T(8,128)(2,1)S(1)} %assemble.1.refs_0_), channel_id=1, source_target_pairs={{0,64},{8,456},{64,128},{72,8},{128,192},{136,72},{192,256},{200,1... | collective-permute-start | bytes 1966088 | tf_op jit(solution)/shard_map/ppermute | solution.py:494
  52.3 17.3 %collective-permute-start.7 = (bf16[80,4096]{1,0:T(8,128)(2,1)}, bf16[80,4096]{1,0:T(8,128)(2,1)}, u32[]{:S(2)}, u32[]{:S(2)}) collective-permute-start(bf16[80,4096]{1,0:T(8,128)(2,1)} %collective-permute-done.4), channel_id=1, source_target_pairs={{0,64},{8,456},{64,128},{72,8},{128,192},{136,72},{192,256},{200,1... | collective-permute-start | bytes 1966088 | tf_op jit(solution)/shard_map/ppermute | solution.py:494
  54.5 11.2 %all-to-all-start.1 = ((f32[8,32,128]{2,1,0:T(8,128)}), f32[8,32,128]{2,1,0:T(8,128)S(1)}, u32[]{:S(2)}, u32[]{:S(2)}) async-start(f32[8,32,128]{2,1,0:T(8,128)} %get-tuple-element.30), calls=%async_computation.1 | async-start | bytes 262144 | tf_op jit(solution)/shard_map/all_to_all | solution.py:499
  59.8 20.6 %copy-start.9 = (bf16[80,4096]{1,0:T(8,128)(2,1)}, bf16[80,4096]{1,0:T(8,128)(2,1)S(1)}, u32[]{:S(2)}) copy-start(bf16[80,4096]{1,0:T(8,128)(2,1)S(1)} %collective-permute-done.3.refs_1_) | copy-start | bytes 1966084
  65.7 3.9 %copy-start.10 = (f32[8,32,128]{2,1,0:T(8,128)}, f32[8,32,128]{2,1,0:T(8,128)S(1)}, u32[]{:S(2)}) copy-start(f32[8,32,128]{2,1,0:T(8,128)S(1)} %all-to-all-done.1) | copy-start | bytes 393220
  65.7 14.7 %collective-permute-start.5 = (bf16[80,4096]{1,0:T(8,128)(2,1)S(1)}, bf16[80,4096]{1,0:T(8,128)(2,1)}, u32[]{:S(2)}, u32[]{:S(2)}) collective-permute-start(bf16[80,4096]{1,0:T(8,128)(2,1)S(1)} %collective-permute-done.3.refs_1_), channel_id=1, source_target_pairs={{0,64},{8,456},{64,128},{72,8},{128,192},{136,72},{192,256},{200,1... | collective-permute-start | bytes 1966088 | tf_op jit(solution)/shard_map/ppermute | solution.py:494
  69.6 18.6 %collective-permute-start.8 = (bf16[80,4096]{1,0:T(8,128)(2,1)}, bf16[80,4096]{1,0:T(8,128)(2,1)S(1)}, u32[]{:S(2)}, u32[]{:S(2)}) collective-permute-start(bf16[80,4096]{1,0:T(8,128)(2,1)} %collective-permute-done.7.refs_2_), channel_id=1, source_target_pairs={{0,64},{8,456},{64,128},{72,8},{128,192},{136,72},{192,256},{200,1... | collective-permute-start | bytes 1966088 | tf_op jit(solution)/shard_map/ppermute | solution.py:494
  80.4 18.6 %collective-permute-start.6 = (bf16[80,4096]{1,0:T(8,128)(2,1)}, bf16[80,4096]{1,0:T(8,128)(2,1)S(1)}, u32[]{:S(2)}, u32[]{:S(2)}) collective-permute-start(bf16[80,4096]{1,0:T(8,128)(2,1)} %collective-permute-done.5.refs_3_), channel_id=1, source_target_pairs={{0,64},{8,456},{64,128},{72,8},{128,192},{136,72},{192,256},{200,1... | collective-permute-start | bytes 1966088 | tf_op jit(solution)/shard_map/ppermute | solution.py:494
  82.3 18.8 %all-to-all-start.2 = ((bf16[8,160,128]{2,1,0:T(8,128)(2,1)}), bf16[8,160,128]{2,1,0:T(8,128)(2,1)S(1)}, u32[]{:S(2)}, u32[]{:S(2)}) async-start(bf16[8,160,128]{2,1,0:T(8,128)(2,1)} %get-tuple-element.36), calls=%async_computation.2 | async-start | bytes 655360 | tf_op jit(solution)/shard_map/all_to_all | solution.py:514
  88.1 13.0 %copy-start.1 = (f32[128,128]{1,0:T(8,128)S(1)}, f32[128,128]{1,0:T(8,128)}, u32[]{:S(2)}) copy-start(f32[128,128]{1,0:T(8,128)} %get-tuple-element.35.refs_3_.refs_2_) | copy-start | bytes 196612
  88.1 3.5 %copy-start.8 = (bf16[80,4096]{1,0:T(8,128)(2,1)}, bf16[80,4096]{1,0:T(8,128)(2,1)S(1)}, u32[]{:S(2)}) copy-start(bf16[80,4096]{1,0:T(8,128)(2,1)S(1)} %collective-permute-done.8.refs_4_) | copy-start | bytes 1966084
  88.2 23.4 %collective-permute-start.9 = (bf16[80,4096]{1,0:T(8,128)(2,1)S(1)}, bf16[80,4096]{1,0:T(8,128)(2,1)S(1)}, u32[]{:S(2)}, u32[]{:S(2)}) collective-permute-start(bf16[80,4096]{1,0:T(8,128)(2,1)S(1)} %collective-permute-done.8.refs_4_), channel_id=1, source_target_pairs={{0,64},{8,456},{64,128},{72,8},{128,192},{136,72},{192,256},{200,1... | collective-permute-start | bytes 1966088 | tf_op jit(solution)/shard_map/ppermute | solution.py:494
  99.0 10.7 %copy-start.14 = (bf16[192,400]{1,0:T(8,128)(2,1)S(1)}, bf16[192,400]{1,0:T(8,128)(2,1)}, u32[]{:S(2)}) copy-start(bf16[192,400]{1,0:T(8,128)(2,1)} %get-tuple-element.41) | copy-start | bytes 460804
  99.0 12.6 %copy-start.5 = (bf16[80,4096]{1,0:T(8,128)(2,1)}, bf16[80,4096]{1,0:T(8,128)(2,1)S(1)}, u32[]{:S(2)}) copy-start(bf16[80,4096]{1,0:T(8,128)(2,1)S(1)} %collective-permute-done.6.refs_0_) | copy-start | bytes 1966084
  99.0 12.6 %collective-permute-start.10 = (bf16[80,4096]{1,0:T(8,128)(2,1)S(1)}, bf16[80,4096]{1,0:T(8,128)(2,1)S(1)}, u32[]{:S(2)}, u32[]{:S(2)}) collective-permute-start(bf16[80,4096]{1,0:T(8,128)(2,1)S(1)} %collective-permute-done.6.refs_0_), channel_id=1, source_target_pairs={{0,64},{8,456},{64,128},{72,8},{128,192},{136,72},{192,256},{200,1... | collective-permute-start | bytes 1966088 | tf_op jit(solution)/shard_map/ppermute | solution.py:494
  102.4 0.6 copy-start.2
  103.0 0.6 copy-start.3
  103.6 18.7 %all-to-all-start.3 = ((bf16[8,160,128]{2,1,0:T(8,128)(2,1)}), bf16[8,160,128]{2,1,0:T(8,128)(2,1)S(1)}, u32[]{:S(2)}, u32[]{:S(2)}) async-start(bf16[8,160,128]{2,1,0:T(8,128)(2,1)} %get-tuple-element.43), calls=%async_computation.3 | async-start | bytes 655360 | tf_op jit(solution)/shard_map/all_to_all | solution.py:522
  109.7 18.8 %collective-permute-start.12 = (bf16[192,400]{1,0:T(8,128)(2,1)S(1)}, bf16[192,400]{1,0:T(8,128)(2,1)S(1)}, u32[]{:S(2)}, u32[]{:S(2)}) collective-permute-start(bf16[192,400]{1,0:T(8,128)(2,1)S(1)} %copy-done.14), channel_id=1, source_target_pairs={{0,8},{8,0},{1,9},{9,1},{2,10},{10,2},{3,11},{11,3},{4,12},{12,4},... | collective-permute-start | bytes 460808 | tf_op jit(solution)/shard_map/ppermute | solution.py:534
  111.6 0.8 copy-start.6
  112.4 0.8 copy-start.7
  117.4 11.0 %collective-permute-start.11 = (bf16[192,240]{1,0:T(8,128)(2,1)}, bf16[192,240]{1,0:T(8,128)(2,1)S(1)}, u32[]{:S(2)}, u32[]{:S(2)}) collective-permute-start(bf16[192,240]{1,0:T(8,128)(2,1)} %expand_other.1), channel_id=1, source_target_pairs={{0,8},{8,0},{1,9},{9,1},{2,10},{10,2},{3,11},{11,3},{4,12},{12,4},... | collective-permute-start | bytes 276488 | tf_op jit(solution)/shard_map/ppermute | solution.py:534
  122.3 0.7 copy-start.11
  128.4 0.6 copy-start.13
  128.4 0.7 copy-start.12
